TPU v7x, 32 devices: a whole 2x2x4 slice. The times are simulated.
32 devices in a mesh: groups: 2 (over x), walker: 16 (over z, y, core).
Axes of the slice: x: 2, y: 2, z: 4, core: 2. Of those that a mesh axis runs over, the one named last changes fastest.
Arguments:
- jacobian_tiles: bfloat16 [32, 192, 2048], P(('groups', 'walker')), parts along dimension 0, may hold values from -6 to 6
Outputs:
- gram: float32 [1536, 768], P(('groups', 'walker')), parts along dimension 0
There are 2 independent parts, one for each index of `groups`. A program takes and returns all parts, laid end to end along the dimension named above; each array names one. Nothing has to cross between parts.
All inputs are finite; a program needn't handle non-finite values.
Results may differ from a plain program's by a relative error of at most 0.0003.
Values may be sent and summed in bfloat16 or wider, within the bound.
No kernel may reach another device: no remote copies, remote signals or barrier semaphores. Data moves between devices by JAX's collectives and lax.ppermute only.
A program may use at most 64 MiB of HBM per device.

v0:
```python
import jax
import jax.numpy as jnp
from jax import lax
from jax.sharding import PartitionSpec as P

PG = 4


def from_behind(block, axis, distance):
    devices = range(lax.axis_size(axis))
    route = [((i - distance) % len(devices), i) for i in devices]
    return lax.ppermute(block, axis, route)


def from_partner(value, axis, bit):
    mask = 2**bit
    pairs = [(source, source ^ mask) for source in range(lax.axis_size(axis))]
    return lax.ppermute(value, axis, pairs)


def shards(jacobian_tiles):
    local_block = jacobian_tiles[0]
    blk_width = local_block.shape[0]
    params_all = local_block.shape[1] * PG
    cycle_len = lax.axis_size("walker") // PG
    my_index = lax.axis_index("walker")
    cycle_pos = my_index // PG
    my_group = my_index % PG
    quarter = blk_width // PG

    def tile_with(moving):
        return lax.dot_general(
            local_block, moving, (((1,), (1,)), ((), ())), preferred_element_type=jnp.float32
        )

    stack_init = jnp.zeros((cycle_len, blk_width, blk_width), jnp.float32)
    stack_init = lax.dynamic_update_index_in_dim(stack_init, tile_with(local_block), 0, 0)

    def advance(step_num, carried):
        moving, tile_stack = carried
        moving = from_behind(moving, "walker", -PG)
        tile_stack = lax.dynamic_update_index_in_dim(tile_stack, tile_with(moving), step_num, 0)
        return (moving, tile_stack)

    unused_block, row_stack = lax.fori_loop(1, cycle_len, advance, (local_block, stack_init))
    for bit_num in range(PG.bit_length() - 2, -1, -1):
        half_rows = row_stack.shape[1] // 2
        my_bit = my_group >> bit_num & 1
        kept_rows = lax.dynamic_slice_in_dim(row_stack, my_bit * half_rows, half_rows, 1)
        sent_rows = lax.dynamic_slice_in_dim(row_stack, (1 - my_bit) * half_rows, half_rows, 1)
        row_stack = kept_rows + from_partner(sent_rows, "walker", bit_num)
    row_stack = jnp.roll(row_stack, cycle_pos, axis=0)
    gram_rows = jnp.transpose(row_stack, (1, 0, 2)).reshape(quarter, cycle_len * blk_width)
    return gram_rows / params_all


def solution(mesh):
    return jax.shard_map(
        shards,
        mesh=mesh,
        in_specs=(P(("groups", "walker"), None, None),),
        out_specs=P(("groups", "walker"), None),
        check_vma=False,
    )
```

profile of v0, /device:TPU:0, one launch (start us, length us, event | category | flops | bytes accessed | tf_op | source)
XLA Modules:
  0.0 76.1 jit_solution(11350187632484869293)
XLA Ops:
  0.0 0.0 copy-start
  0.0 1.8 %convolution_bitcast_fusion.1 = f32[1,192,192]{2,1,0:T(8,128)S(1)} fusion(bf16[1,192,2048]{2,1,0:T(8,128)(2,1)} %param.3), kind=kOutput, calls=%fused_computation.2 | convolution fusion | flops 150994944 | bytes 933888 | tf_op jit(solution)/shard_map/dot_general | solution.py:32
  1.8 0.0 copy-done
  1.8 0.1 copy.5
  1.9 0.1 dynamic_update_slice.14
  2.0 63.1 %while.17 = (s32[]{:T(128)}, bf16[192,2048]{1,0:T(8,128)(2,1)S(1)}, f32[4,192,192]{2,1,0:T(8,128)S(1)}, bf16[192,2048]{1,0:T(8,128)(2,1)S(1)}, s32[]{:T(128)}, /*index=5*/s32[]{:T(128)}, s32[]{:T(128)}) while((s32[]{:T(128)}, bf16[192,2048]{1,0:T(8,128)(2,1)S(1)}, f32[4,192,192]{2,1,0:T(8,128)S(1)}, bf16[192,2048]{1,0:T(8,128)(2,1)S(1)}, ...), condition=%wide.region_1.2_spmd, body=%wide.region_0.1_spmd.sunk | while | flops 150994944 | bytes 6488227 | solution.py:45
  2.0 5.1 %collective-permute-start = (bf16[192,2048]{1,0:T(8,128)(2,1)S(1)}, bf16[192,2048]{1,0:T(8,128)(2,1)S(1)}, u32[]{:S(2)}, u32[]{:S(2)}) collective-permute-start(bf16[192,2048]{1,0:T(8,128)(2,1)S(1)} %get-tuple-element.157), channel_id=1, source_target_pairs={{4,0},{5,1},{6,2},{7,3},{8,4},{9,5},{10,6},{11,7},{12,8},{13,9},{1... | collective-permute-start | bytes 2359304 | tf_op jit(solution)/shard_map/while/body/eval_jaxpr/ppermute | solution.py:12
  7.1 16.8 %collective-permute-done = bf16[192,2048]{1,0:T(8,128)(2,1)S(1)} collective-permute-done((bf16[192,2048]{1,0:T(8,128)(2,1)S(1)}, bf16[192,2048]{1,0:T(8,128)(2,1)S(1)}, u32[]{:S(2)}, u32[]{:S(2)}) %collective-permute-start) | collective-permute-done | bytes 786464 | tf_op jit(solution)/shard_map/while/body/eval_jaxpr/ppermute | solution.py:12
  23.9 0.1 copy.11
  24.0 0.4 fusion.12
  24.4 4.3 %collective-permute-start = (bf16[192,2048]{1,0:T(8,128)(2,1)S(1)}, bf16[192,2048]{1,0:T(8,128)(2,1)S(1)}, u32[]{:S(2)}, u32[]{:S(2)}) collective-permute-start(bf16[192,2048]{1,0:T(8,128)(2,1)S(1)} %get-tuple-element.157), channel_id=1, source_target_pairs={{4,0},{5,1},{6,2},{7,3},{8,4},{9,5},{10,6},{11,7},{12,8},{13,9},{1... | collective-permute-start | bytes 2359304 | tf_op jit(solution)/shard_map/while/body/eval_jaxpr/ppermute | solution.py:12
  28.8 15.9 %collective-permute-done = bf16[192,2048]{1,0:T(8,128)(2,1)S(1)} collective-permute-done((bf16[192,2048]{1,0:T(8,128)(2,1)S(1)}, bf16[192,2048]{1,0:T(8,128)(2,1)S(1)}, u32[]{:S(2)}, u32[]{:S(2)}) %collective-permute-start) | collective-permute-done | bytes 786464 | tf_op jit(solution)/shard_map/while/body/eval_jaxpr/ppermute | solution.py:12
  44.7 0.1 copy.11
  44.8 0.4 fusion.12
  45.2 4.3 %collective-permute-start = (bf16[192,2048]{1,0:T(8,128)(2,1)S(1)}, bf16[192,2048]{1,0:T(8,128)(2,1)S(1)}, u32[]{:S(2)}, u32[]{:S(2)}) collective-permute-start(bf16[192,2048]{1,0:T(8,128)(2,1)S(1)} %get-tuple-element.157), channel_id=1, source_target_pairs={{4,0},{5,1},{6,2},{7,3},{8,4},{9,5},{10,6},{11,7},{12,8},{13,9},{1... | collective-permute-start | bytes 2359304 | tf_op jit(solution)/shard_map/while/body/eval_jaxpr/ppermute | solution.py:12
  49.5 15.1 %collective-permute-done = bf16[192,2048]{1,0:T(8,128)(2,1)S(1)} collective-permute-done((bf16[192,2048]{1,0:T(8,128)(2,1)S(1)}, bf16[192,2048]{1,0:T(8,128)(2,1)S(1)}, u32[]{:S(2)}, u32[]{:S(2)}) %collective-permute-start) | collective-permute-done | bytes 786464 | tf_op jit(solution)/shard_map/while/body/eval_jaxpr/ppermute | solution.py:12
  64.6 0.1 copy.11
  64.7 0.4 fusion.12
  65.1 1.6 %collective-permute-start.1 = (f32[4,96,192]{2,1,0:T(8,128)S(1)}, f32[4,96,192]{2,1,0:T(8,128)S(1)}, u32[]{:S(2)}, u32[]{:S(2)}) collective-permute-start(f32[4,96,192]{2,1,0:T(8,128)S(1)} %constant_dynamic-slice_fusion.1), channel_id=1, source_target_pairs={{0,2},{1,3},{2,0},{3,1},{4,6},{5,7},{6,4},{7,5},{8,10},{9,11},{10,... | collective-permute-start | bytes 884744 | tf_op jit(solution)/shard_map/ppermute | solution.py:18
  66.7 6.8 %collective-permute-done.1 = f32[4,96,192]{2,1,0:T(8,128)S(1)} collective-permute-done((f32[4,96,192]{2,1,0:T(8,128)S(1)}, f32[4,96,192]{2,1,0:T(8,128)S(1)}, u32[]{:S(2)}, u32[]{:S(2)}) %collective-permute-start.1) | collective-permute-done | bytes 294944 | tf_op jit(solution)/shard_map/ppermute | solution.py:18
  73.5 0.1 dynamic-slice_add_fusion
  73.6 0.1 collective-permute-start.2
  73.7 1.4 %collective-permute-done.2 = f32[4,48,192]{2,1,0:T(8,128)S(1)} collective-permute-done((f32[4,48,192]{2,1,0:T(8,128)S(1)}, f32[4,48,192]{2,1,0:T(8,128)S(1)}, u32[]{:S(2)}, u32[]{:S(2)}) %collective-permute-start.2) | collective-permute-done | bytes 147488 | tf_op jit(solution)/shard_map/ppermute | solution.py:18
  75.1 0.1 fusion.3
  75.2 0.1 copy.2
  75.3 0.8 %div.24 = f32[48,768]{1,0:T(8,128)} reshape(f32[48,4,192]{2,1,0:T(4,128)S(1)} %copy.2) | data formatting | bytes 294912 | tf_op jit(solution)/shard_map/div | solution.py:54
  (3 shorter events, 0.1 us)
Async XLA Ops:
  0.0 1.8 %copy-start = (bf16[1,192,2048]{2,1,0:T(8,128)(2,1)S(1)}, bf16[1,192,2048]{2,1,0:T(8,128)(2,1)}, u32[]{:S(2)}) copy-start(bf16[1,192,2048]{2,1,0:T(8,128)(2,1)} %param.3) | copy-start | bytes 2359300
  2.0 21.9 %collective-permute-start = (bf16[192,2048]{1,0:T(8,128)(2,1)S(1)}, bf16[192,2048]{1,0:T(8,128)(2,1)S(1)}, u32[]{:S(2)}, u32[]{:S(2)}) collective-permute-start(bf16[192,2048]{1,0:T(8,128)(2,1)S(1)} %get-tuple-element.157), channel_id=1, source_target_pairs={{4,0},{5,1},{6,2},{7,3},{8,4},{9,5},{10,6},{11,7},{12,8},{13,9},{1... | collective-permute-start | bytes 2359304 | tf_op jit(solution)/shard_map/while/body/eval_jaxpr/ppermute | solution.py:12
  24.4 20.3 %collective-permute-start = (bf16[192,2048]{1,0:T(8,128)(2,1)S(1)}, bf16[192,2048]{1,0:T(8,128)(2,1)S(1)}, u32[]{:S(2)}, u32[]{:S(2)}) collective-permute-start(bf16[192,2048]{1,0:T(8,128)(2,1)S(1)} %get-tuple-element.157), channel_id=1, source_target_pairs={{4,0},{5,1},{6,2},{7,3},{8,4},{9,5},{10,6},{11,7},{12,8},{13,9},{1... | collective-permute-start | bytes 2359304 | tf_op jit(solution)/shard_map/while/body/eval_jaxpr/ppermute | solution.py:12
  45.2 19.4 %collective-permute-start = (bf16[192,2048]{1,0:T(8,128)(2,1)S(1)}, bf16[192,2048]{1,0:T(8,128)(2,1)S(1)}, u32[]{:S(2)}, u32[]{:S(2)}) collective-permute-start(bf16[192,2048]{1,0:T(8,128)(2,1)S(1)} %get-tuple-element.157), channel_id=1, source_target_pairs={{4,0},{5,1},{6,2},{7,3},{8,4},{9,5},{10,6},{11,7},{12,8},{13,9},{1... | collective-permute-start | bytes 2359304 | tf_op jit(solution)/shard_map/while/body/eval_jaxpr/ppermute | solution.py:12
  65.1 8.3 %collective-permute-start.1 = (f32[4,96,192]{2,1,0:T(8,128)S(1)}, f32[4,96,192]{2,1,0:T(8,128)S(1)}, u32[]{:S(2)}, u32[]{:S(2)}) collective-permute-start(f32[4,96,192]{2,1,0:T(8,128)S(1)} %constant_dynamic-slice_fusion.1), channel_id=1, source_target_pairs={{0,2},{1,3},{2,0},{3,1},{4,6},{5,7},{6,4},{7,5},{8,10},{9,11},{10,... | collective-permute-start | bytes 884744 | tf_op jit(solution)/shard_map/ppermute | solution.py:18
  73.6 1.5 %collective-permute-start.2 = (f32[4,48,192]{2,1,0:T(8,128)S(1)}, f32[4,48,192]{2,1,0:T(8,128)S(1)}, u32[]{:S(2)}, u32[]{:S(2)}) collective-permute-start(f32[4,48,192]{2,1,0:T(8,128)S(1)} %constant_dynamic-slice_fusion), channel_id=1, source_target_pairs={{0,1},{1,0},{2,3},{3,2},{4,5},{5,4},{6,7},{7,6},{8,9},{9,8},{10,11... | collective-permute-start | bytes 442376 | tf_op jit(solution)/shard_map/ppermute | solution.py:18
where the time goes:
time: 76.2 us; the launch traced here: 76.1 us
  waiting for transfers between devices  56 us (73%)
  starting transfers between devices  15.4 us (20%)
  matrix products  3 us (4%)
  local copies, waits for them, and re-layouts  1.32 us (2%)
    ppermute x3, waiting for transfers between devices, from_behind(): return lax.ppermute(block, axis, route)  47.8 us
    ppermute x3, starting transfers between devices, from_behind(): return lax.ppermute(block, axis, route)  13.8 us
    ppermute x2, waiting for transfers between devices, from_partner(): return lax.ppermute(value, axis, pairs)  8.15 us
    dot_general x4, matrix products, tile_with(): lax.dot_general(local_block, moving, (((1,), (1,)), ((), ())), preferred_...  3 us
    ppermute x2, starting transfers between devices, from_partner(): return lax.ppermute(value, axis, pairs)  1.66 us
  transfers between devices with their start and end apart: 5, of which 5 were waited for; matrix products, arithmetic and copies ran while one was open for 0% of the time, Pallas kernels for 0%

commit v1 on v0

--- a/solution.py
+++ b/solution.py
@@ -3,7 +3,92 @@
 from jax import lax
 from jax.sharding import PartitionSpec as P
 
+
 PG = 4
+
+
+def dot(a, b):
+    return lax.dot_general(a, b, (((1,), (1,)), ((), ())), preferred_element_type=jnp.float32)
+
+
+def line(jacobian_tiles):
+    return body(jacobian_tiles)
+
+
+def body(jacobian_tiles):
+    own = jacobian_tiles[0]
+    width, cols = own.shape
+    n = lax.axis_size("walker") // PG
+    ring = 2 * n
+    quarter = width // PG
+    me = lax.axis_index("walker")
+    pos, group = me // PG, me % PG
+    side, core = group // 2, group % 2
+
+    def device(r, y):
+        r = r % ring
+        return r * PG + 2 * y if r < n else (ring - 1 - r) * PG + 2 * y + 1
+
+    def move(value, step, flip=0, only=None):
+        pairs = [
+            (device(r, y), device(r + step, y ^ flip))
+            for y in range(2)
+            for r in range(ring)
+            if only is None or r % n in only
+        ]
+        return lax.ppermute(value, "walker", pairs)
+
+    k = cols // 2
+    own_parts = [own[:, :k], own[:, k:]]
+    a_parts = [move(part, 1) for part in own_parts]
+    b_parts = [move(part, 1, only=(1, 2, 3)) for part in a_parts]
+    p = move(own, -1, only=(3,))
+
+    def halves(block):
+        block = block.reshape(2, width // 2, width)
+        return (
+            lax.dynamic_index_in_dim(block, side, 0, False),
+            lax.dynamic_index_in_dim(block, 1 - side, 0, False),
+        )
+
+    def both(xs, ys):
+        return dot(xs[0], ys[0]) + dot(xs[1], ys[1])
+
+    s1 = both(own_parts, own_parts)
+    s2 = both(own_parts, a_parts)
+    s2t = both(a_parts, own_parts)
+    keep, send = zip(*(halves(s) for s in (s1, s2, s2t)))
+    early = jnp.stack(keep) + move(jnp.stack(send), 0, 1)
+    up1 = move(early[2], -1)
+
+    p_parts = [p[:, :k], p[:, k:]]
+    s3 = both(own_parts, b_parts)
+    s3t = both(b_parts, own_parts)
+    s4 = both(b_parts, p_parts)
+    s4t = both(p_parts, b_parts)
+    s3k, s3s = halves(s3)
+    down2 = s3k + move(s3s, 0, 1)
+    tk, ts = halves(s3t)
+    up2 = move(tk, -2) + move(ts, -2, 1)
+    fk, fs = halves(s4)
+    up3 = move(fk, -2, only=(2,)) + move(fs, -2, 1, only=(2,))
+    gk, gs = halves(s4t)
+    down3 = move(gk, 1, only=(2,)) + move(gs, 1, 1, only=(2,))
+    found = {0: early[0], -1: early[1], 1: up1, -2: down2, 2: up2, -3: down3, 3: up3}
+    sign = 1 - 2 * core
+    blocks = []
+    for b in range(n):
+        offset = sign * (b - pos)
+        value = found[0]
+        for d, v in found.items():
+            if d:
+                value = jnp.where(offset == d, v, value)
+        blocks.append(value)
+    rows = jnp.stack(blocks, 1).reshape(2, quarter, n * width)
+    mine = lax.dynamic_index_in_dim(rows, core, 0, False)
+    theirs = lax.dynamic_index_in_dim(rows, 1 - core, 0, False)
+    pairs = [(i, i ^ 1) for i in range(n * PG)]
+    return (mine + lax.ppermute(theirs, "walker", pairs)) / (cols * PG)
 
 
 def from_behind(block, axis, distance):
@@ -18,7 +103,7 @@
     return lax.ppermute(value, axis, pairs)
 
 
-def shards(jacobian_tiles):
+def long_line(jacobian_tiles):
     local_block = jacobian_tiles[0]
     blk_width = local_block.shape[0]
     params_all = local_block.shape[1] * PG
@@ -42,7 +127,7 @@
         tile_stack = lax.dynamic_update_index_in_dim(tile_stack, tile_with(moving), step_num, 0)
         return (moving, tile_stack)
 
-    unused_block, row_stack = lax.fori_loop(1, cycle_len, advance, (local_block, stack_init))
+    _, row_stack = lax.fori_loop(1, cycle_len, advance, (local_block, stack_init))
     for bit_num in range(PG.bit_length() - 2, -1, -1):
         half_rows = row_stack.shape[1] // 2
         my_bit = my_group >> bit_num & 1
@@ -54,9 +139,13 @@
     return gram_rows / params_all
 
 
+SPAN = 4
+
+
 def solution(mesh):
+    meets = mesh.shape["walker"] == SPAN * PG
     return jax.shard_map(
-        shards,
+        line if meets else long_line,
         mesh=mesh,
         in_specs=(P(("groups", "walker"), None, None),),
         out_specs=P(("groups", "walker"), None),

time: 76.2 us -> 55.7 us (0.73)
  waiting for transfers between devices: 56 us -> 22.5 us
  starting transfers between devices: 15.4 us -> 25.2 us
  other arithmetic: 0.13 us -> 1.36 us
  matrix products: 3 us -> 4.01 us
    ppermute x5 -> x15, waiting for transfers between devices: 56 us -> 22.5 us  [the longest x14 21.2 us: move(): return lax.ppermute(value, 'walker', pairs)]
    ppermute x5 -> x15, starting transfers between devices: 15.4 us -> 25.2 us  [the longest x14 25 us: move(): return lax.ppermute(value, 'walker', pairs)]
    slice x0 -> x1, local copies, waits for them, and re-layouts: none -> 1.17 us  [body(): own_parts = [own[:, :k], own[:, k:]]]
    dot_general x4 -> x14, matrix products: 3 us -> 4.01 us  [dot(): lax.dot_general(a, b, (((1,), (1,)), ((), ())), preferred_element_type=jn...]
    div x2 -> x0, local copies, waits for them, and re-layouts: 0.93 us -> none  [shards(): return gram_rows / params_all]
  transfers between devices with their start and end apart: 5 -> 15, of which waited for: 5 -> 8; matrix products, arithmetic and copies ran while one was open for 0% -> 10% of each run, Pallas kernels for 0% -> 0%
where the time goes in v1:
time: 55.7 us; the launch traced here: 55.4 us
  starting transfers between devices  25.2 us (45%)
  waiting for transfers between devices  22.5 us (40%)
  matrix products  4.01 us (7%)
  local copies, waits for them, and re-layouts  1.97 us (4%)
  other arithmetic  1.36 us (2%)
    ppermute x14, starting transfers between devices, move(): return lax.ppermute(value, 'walker', pairs)  25 us
    ppermute x14, waiting for transfers between devices, move(): return lax.ppermute(value, 'walker', pairs)  21.2 us
    dot_general x14, matrix products, dot(): lax.dot_general(a, b, (((1,), (1,)), ((), ())), preferred_element_type=jn...  4.01 us
    ppermute x1, waiting for transfers between devices, body(): return (mine + lax.ppermute(theirs, 'walker', pairs)) / (cols * PG)  1.25 us
    slice x1, local copies, waits for them, and re-layouts, body(): own_parts = [own[:, :k], own[:, k:]]  1.17 us
  transfers between devices with their start and end apart: 15, of which 8 were waited for; matrix products, arithmetic and copies ran while one was open for 10% of the time, Pallas kernels for 0%

profile of v1, /device:TPU:0, one launch (start us, length us, event | category | flops | bytes accessed | tf_op | source)
XLA Modules:
  0.0 55.4 jit_solution(6160733784594151710)
XLA Ops:
  0.0 0.0 copy-start
  0.0 0.8 %collective-permute-start.2 = (bf16[192,2048]{1,0:T(8,128)(2,1)}, bf16[192,2048]{1,0:T(8,128)(2,1)S(1)}, u32[]{:S(2)}, u32[]{:S(2)}) collective-permute-start(bf16[192,2048]{1,0:T(8,128)(2,1)} %bitcast.97), channel_id=1, source_target_pairs={{12,8},{1,5},{14,10},{3,7},{28,24},{17,21},{30,26},{19,23}} | collective-permute-start | bytes 2359304 | tf_op jit(solution)/shard_map/ppermute | solution.py:39
  0.8 1.2 %fusion.41 = (bf16[192,1024]{1,0:T(8,128)(2,1)S(1)}, bf16[192,1024]{1,0:T(8,128)(2,1)S(1)}) fusion(bf16[192,2048]{1,0:T(8,128)(2,1)} %bitcast.98), kind=kLoop, calls=%fused_computation.72 | loop fusion | bytes 1572864 | tf_op jit(solution)/shard_map/slice | solution.py:42
  2.0 3.1 %collective-permute-start.3 = (bf16[192,1024]{1,0:T(8,128)(2,1)S(1)}, bf16[192,1024]{1,0:T(8,128)(2,1)S(1)}, u32[]{:S(2)}, u32[]{:S(2)}) collective-permute-start(bf16[192,1024]{1,0:T(8,128)(2,1)S(1)} %get-tuple-element.11), channel_id=1, source_target_pairs={{0,4},{4,8},{8,12},{12,13},{13,9},{9,5},{5,1},{1,0},{2,6},{6,10},{... | collective-permute-start | bytes 1179656 | tf_op jit(solution)/shard_map/ppermute | solution.py:39
  5.1 2.2 %collective-permute-start = (bf16[192,1024]{1,0:T(8,128)(2,1)S(1)}, bf16[192,1024]{1,0:T(8,128)(2,1)S(1)}, u32[]{:S(2)}, u32[]{:S(2)}) collective-permute-start(bf16[192,1024]{1,0:T(8,128)(2,1)S(1)} %get-tuple-element.10), channel_id=1, source_target_pairs={{0,4},{4,8},{8,12},{12,13},{13,9},{9,5},{5,1},{1,0},{2,6},{6,10},{... | collective-permute-start | bytes 1179656 | tf_op jit(solution)/shard_map/ppermute | solution.py:39
  7.2 0.0 copy-done
  7.2 0.3 fusion.37
  7.6 0.3 convolution_add_fusion.2
  7.9 6.7 %collective-permute-done.3 = bf16[192,1024]{1,0:T(8,128)(2,1)S(1)} collective-permute-done((bf16[192,1024]{1,0:T(8,128)(2,1)S(1)}, bf16[192,1024]{1,0:T(8,128)(2,1)S(1)}, u32[]{:S(2)}, u32[]{:S(2)}) %collective-permute-start.3) | collective-permute-done | bytes 393248 | tf_op jit(solution)/shard_map/ppermute | solution.py:39
  14.6 0.3 fusion.28
  14.9 0.3 fusion.26
  15.2 6.9 %collective-permute-done = bf16[192,1024]{1,0:T(8,128)(2,1)S(1)} collective-permute-done((bf16[192,1024]{1,0:T(8,128)(2,1)S(1)}, bf16[192,1024]{1,0:T(8,128)(2,1)S(1)}, u32[]{:S(2)}, u32[]{:S(2)}) %collective-permute-start) | collective-permute-done | bytes 393248 | tf_op jit(solution)/shard_map/ppermute | solution.py:39
  22.1 0.3 convolution_add_fusion.1
  22.4 0.3 convolution_add_fusion
  22.7 1.6 %collective-permute-start.12 = (f32[3,96,192]{2,1,0:T(8,128)S(1)}, f32[3,96,192]{2,1,0:T(8,128)S(1)}, u32[]{:S(2)}, u32[]{:S(2)}) collective-permute-start(f32[3,96,192]{2,1,0:T(8,128)S(1)} %pad_maximum_fusion.1), channel_id=1, source_target_pairs={{0,2},{4,6},{8,10},{12,14},{13,15},{9,11},{5,7},{1,3},{2,0},{6,4},... | collective-permute-start | bytes 663560 | tf_op jit(solution)/shard_map/ppermute | solution.py:39
  24.3 1.3 %collective-permute-start.4 = (bf16[192,1024]{1,0:T(8,128)(2,1)S(1)}, bf16[192,1024]{1,0:T(8,128)(2,1)S(1)}, u32[]{:S(2)}, u32[]{:S(2)}) collective-permute-start(bf16[192,1024]{1,0:T(8,128)(2,1)S(1)} %collective-permute-done.3), channel_id=1, source_target_pairs={{4,8},{8,12},{12,13},{9,5},{5,1},{1,0},{6,10},{10,14},{14,15},{11,... | collective-permute-start | bytes 1179656 | tf_op jit(solution)/shard_map/ppermute | solution.py:39
  25.6 1.3 %collective-permute-start.1 = (bf16[192,1024]{1,0:T(8,128)(2,1)S(1)}, bf16[192,1024]{1,0:T(8,128)(2,1)S(1)}, u32[]{:S(2)}, u32[]{:S(2)}) collective-permute-start(bf16[192,1024]{1,0:T(8,128)(2,1)S(1)} %collective-permute-done), channel_id=1, source_target_pairs={{4,8},{8,12},{12,13},{9,5},{5,1},{1,0},{6,10},{10,14},{14,15},{11,... | collective-permute-start | bytes 1179656 | tf_op jit(solution)/shard_map/ppermute | solution.py:39
  26.9 2.6 %collective-permute-done.12 = f32[3,96,192]{2,1,0:T(8,128)S(1)} collective-permute-done((f32[3,96,192]{2,1,0:T(8,128)S(1)}, f32[3,96,192]{2,1,0:T(8,128)S(1)}, u32[]{:S(2)}, u32[]{:S(2)}) %collective-permute-start.12) | collective-permute-done | bytes 221216 | tf_op jit(solution)/shard_map/ppermute | solution.py:39
  29.6 0.0 collective-permute-start.13
  29.6 0.0 collective-permute-done.4
  29.6 0.0 collective-permute-done.2
  29.6 0.3 fusion.2
  29.9 0.0 collective-permute-done.1
  29.9 0.3 convolution_add_fusion.6
  30.3 1.3 %collective-permute-start.5 = (f32[96,192]{1,0:T(8,128)S(1)}, f32[96,192]{1,0:T(8,128)S(1)}, u32[]{:S(2)}, u32[]{:S(2)}) collective-permute-start(f32[96,192]{1,0:T(8,128)S(1)} %get-tuple-element.13), channel_id=1, source_target_pairs={{8,0},{5,13},{10,2},{7,15},{24,16},{21,29},{26,18},{23,31}} | collective-permute-start | bytes 221192 | tf_op jit(solution)/shard_map/ppermute | solution.py:39
  31.6 1.3 %collective-permute-start.6 = (f32[96,192]{1,0:T(8,128)S(1)}, f32[96,192]{1,0:T(8,128)S(1)}, u32[]{:S(2)}, u32[]{:S(2)}) collective-permute-start(f32[96,192]{1,0:T(8,128)S(1)} %get-tuple-element.12), channel_id=1, source_target_pairs={{8,2},{5,15},{10,0},{7,13},{24,18},{21,31},{26,16},{23,29}} | collective-permute-start | bytes 221192 | tf_op jit(solution)/shard_map/ppermute | solution.py:39
  32.9 0.3 fusion
  33.2 0.3 convolution_add_fusion.5
  33.5 0.7 %collective-permute-start.7 = (f32[96,192]{1,0:T(8,128)S(1)}, f32[96,192]{1,0:T(8,128)S(1)}, u32[]{:S(2)}, u32[]{:S(2)}) collective-permute-start(f32[96,192]{1,0:T(8,128)S(1)} %get-tuple-element.15), channel_id=1, source_target_pairs={{8,12},{5,1},{10,14},{7,3},{24,28},{21,17},{26,30},{23,19}} | collective-permute-start | bytes 221192 | tf_op jit(solution)/shard_map/ppermute | solution.py:39
  34.2 0.7 %collective-permute-start.8 = (f32[96,192]{1,0:T(8,128)S(1)}, f32[96,192]{1,0:T(8,128)S(1)}, u32[]{:S(2)}, u32[]{:S(2)}) collective-permute-start(f32[96,192]{1,0:T(8,128)S(1)} %get-tuple-element.14), channel_id=1, source_target_pairs={{8,14},{5,3},{10,12},{7,1},{24,30},{21,19},{26,28},{23,17}} | collective-permute-start | bytes 221192 | tf_op jit(solution)/shard_map/ppermute | solution.py:39
  34.8 0.3 fusion.33
  35.1 0.3 convolution_add_fusion.4
  35.5 0.3 fusion.31
  35.8 0.3 convolution_add_fusion.3
  36.1 0.0 collective-permute-done.13
  36.1 9.3 %collective-permute-start.10 = (f32[96,192]{1,0:T(8,128)S(1)}, f32[96,192]{1,0:T(8,128)S(1)}, u32[]{:S(2)}, u32[]{:S(2)}) collective-permute-start(f32[96,192]{1,0:T(8,128)S(1)} %get-tuple-element.16), channel_id=1, source_target_pairs={{0,7},{4,3},{8,2},{12,6},{13,10},{9,14},{5,15},{1,11},{2,5},{6,1},... | collective-permute-start | bytes 221192 | tf_op jit(solution)/shard_map/ppermute | solution.py:39
  45.4 0.0 collective-permute-done.5
  45.4 0.0 collective-permute-start.9
  45.4 0.6 %collective-permute-done.6 = f32[96,192]{1,0:T(8,128)S(1)} collective-permute-done((f32[96,192]{1,0:T(8,128)S(1)}, f32[96,192]{1,0:T(8,128)S(1)}, u32[]{:S(2)}, u32[]{:S(2)}) %collective-permute-start.6) | collective-permute-done | bytes 73760 | tf_op jit(solution)/shard_map/ppermute | solution.py:39
  46.0 1.5 %collective-permute-start.11 = (f32[96,192]{1,0:T(8,128)S(1)}, f32[96,192]{1,0:T(8,128)S(1)}, u32[]{:S(2)}, u32[]{:S(2)}) collective-permute-start(f32[96,192]{1,0:T(8,128)S(1)} %dynamic-slice_bitcast_fusion.1), channel_id=1, source_target_pairs={{0,2},{4,6},{8,10},{12,14},{13,15},{9,11},{5,7},{1,3},{2,0},{6,4},... | collective-permute-start | bytes 221192 | tf_op jit(solution)/shard_map/ppermute | solution.py:39
  47.5 0.0 collective-permute-done.7
  47.5 0.0 collective-permute-done.8
  47.5 4.1 %collective-permute-done.10 = f32[96,192]{1,0:T(8,128)S(1)} collective-permute-done((f32[96,192]{1,0:T(8,128)S(1)}, f32[96,192]{1,0:T(8,128)S(1)}, u32[]{:S(2)}, u32[]{:S(2)}) %collective-permute-start.10) | collective-permute-done | bytes 73760 | tf_op jit(solution)/shard_map/ppermute | solution.py:39
  51.7 0.1 collective-permute-done.9
  51.8 0.2 collective-permute-done.11
  51.9 0.1 fusion.25
  52.1 0.1 copy.3
  52.2 0.1 copy.4
  52.4 0.1 stack.32
  52.5 0.1 copy.2
  52.6 0.4 pad_maximum_fusion
  53.0 0.2 reshape.39
  53.3 0.2 collective-permute-start.14
  53.5 1.3 %collective-permute-done.14 = f32[48,768]{1,0:T(8,128)S(1)} collective-permute-done((f32[48,768]{1,0:T(8,128)S(1)}, f32[48,768]{1,0:T(8,128)S(1)}, u32[]{:S(2)}, u32[]{:S(2)}) %collective-permute-start.14) | collective-permute-done | bytes 147488 | tf_op jit(solution)/shard_map/ppermute | solution.py:91
  54.7 0.7 %fusion.6 = f32[48,768]{1,0:T(8,128)} fusion(f32[48,768]{1,0:T(8,128)S(1)} %collective-permute-done.14, f32[2,48,768]{2,1,0:T(8,128)S(1)} %reshape.39, s32[]{:T(128)S(6)} %select_n.260), kind=kLoop, calls=%fused_computation.17 | loop fusion | flops 73728 | bytes 442372 | tf_op jit(solution)/shard_map/div | solution.py:91
  (13 shorter events, 0.4 us)
Async XLA Ops:
  0.0 7.2 %copy-start = (bf16[1,192,2048]{2,1,0:T(8,128)(2,1)S(1)}, bf16[1,192,2048]{2,1,0:T(8,128)(2,1)}, u32[]{:S(2)}) copy-start(bf16[1,192,2048]{2,1,0:T(8,128)(2,1)} %param.1) | copy-start | bytes 2359300
  0.0 29.6 %collective-permute-start.2 = (bf16[192,2048]{1,0:T(8,128)(2,1)}, bf16[192,2048]{1,0:T(8,128)(2,1)S(1)}, u32[]{:S(2)}, u32[]{:S(2)}) collective-permute-start(bf16[192,2048]{1,0:T(8,128)(2,1)} %bitcast.97), channel_id=1, source_target_pairs={{12,8},{1,5},{14,10},{3,7},{28,24},{17,21},{30,26},{19,23}} | collective-permute-start | bytes 2359304 | tf_op jit(solution)/shard_map/ppermute | solution.py:39
  2.0 12.6 %collective-permute-start.3 = (bf16[192,1024]{1,0:T(8,128)(2,1)S(1)}, bf16[192,1024]{1,0:T(8,128)(2,1)S(1)}, u32[]{:S(2)}, u32[]{:S(2)}) collective-permute-start(bf16[192,1024]{1,0:T(8,128)(2,1)S(1)} %get-tuple-element.11), channel_id=1, source_target_pairs={{0,4},{4,8},{8,12},{12,13},{13,9},{9,5},{5,1},{1,0},{2,6},{6,10},{... | collective-permute-start | bytes 1179656 | tf_op jit(solution)/shard_map/ppermute | solution.py:39
  5.1 17.0 %collective-permute-start = (bf16[192,1024]{1,0:T(8,128)(2,1)S(1)}, bf16[192,1024]{1,0:T(8,128)(2,1)S(1)}, u32[]{:S(2)}, u32[]{:S(2)}) collective-permute-start(bf16[192,1024]{1,0:T(8,128)(2,1)S(1)} %get-tuple-element.10), channel_id=1, source_target_pairs={{0,4},{4,8},{8,12},{12,13},{13,9},{9,5},{5,1},{1,0},{2,6},{6,10},{... | collective-permute-start | bytes 1179656 | tf_op jit(solution)/shard_map/ppermute | solution.py:39
  22.7 6.8 %collective-permute-start.12 = (f32[3,96,192]{2,1,0:T(8,128)S(1)}, f32[3,96,192]{2,1,0:T(8,128)S(1)}, u32[]{:S(2)}, u32[]{:S(2)}) collective-permute-start(f32[3,96,192]{2,1,0:T(8,128)S(1)} %pad_maximum_fusion.1), channel_id=1, source_target_pairs={{0,2},{4,6},{8,10},{12,14},{13,15},{9,11},{5,7},{1,3},{2,0},{6,4},... | collective-permute-start | bytes 663560 | tf_op jit(solution)/shard_map/ppermute | solution.py:39
  24.3 5.3 %collective-permute-start.4 = (bf16[192,1024]{1,0:T(8,128)(2,1)S(1)}, bf16[192,1024]{1,0:T(8,128)(2,1)S(1)}, u32[]{:S(2)}, u32[]{:S(2)}) collective-permute-start(bf16[192,1024]{1,0:T(8,128)(2,1)S(1)} %collective-permute-done.3), channel_id=1, source_target_pairs={{4,8},{8,12},{12,13},{9,5},{5,1},{1,0},{6,10},{10,14},{14,15},{11,... | collective-permute-start | bytes 1179656 | tf_op jit(solution)/shard_map/ppermute | solution.py:39
  25.6 4.3 %collective-permute-start.1 = (bf16[192,1024]{1,0:T(8,128)(2,1)S(1)}, bf16[192,1024]{1,0:T(8,128)(2,1)S(1)}, u32[]{:S(2)}, u32[]{:S(2)}) collective-permute-start(bf16[192,1024]{1,0:T(8,128)(2,1)S(1)} %collective-permute-done), channel_id=1, source_target_pairs={{4,8},{8,12},{12,13},{9,5},{5,1},{1,0},{6,10},{10,14},{14,15},{11,... | collective-permute-start | bytes 1179656 | tf_op jit(solution)/shard_map/ppermute | solution.py:39
  29.6 6.5 %collective-permute-start.13 = (f32[96,192]{1,0:T(8,128)S(1)}, f32[96,192]{1,0:T(8,128)S(1)}, u32[]{:S(2)}, u32[]{:S(2)}) collective-permute-start(f32[96,192]{1,0:T(8,128)S(1)} %slice_bitcast_fusion), channel_id=1, source_target_pairs={{0,1},{4,0},{8,4},{12,8},{13,12},{9,13},{5,9},{1,5},{2,3},{6,2},{1... | collective-permute-start | bytes 221192 | tf_op jit(solution)/shard_map/ppermute | solution.py:39
  30.3 15.1 %collective-permute-start.5 = (f32[96,192]{1,0:T(8,128)S(1)}, f32[96,192]{1,0:T(8,128)S(1)}, u32[]{:S(2)}, u32[]{:S(2)}) collective-permute-start(f32[96,192]{1,0:T(8,128)S(1)} %get-tuple-element.13), channel_id=1, source_target_pairs={{8,0},{5,13},{10,2},{7,15},{24,16},{21,29},{26,18},{23,31}} | collective-permute-start | bytes 221192 | tf_op jit(solution)/shard_map/ppermute | solution.py:39
  31.6 14.4 %collective-permute-start.6 = (f32[96,192]{1,0:T(8,128)S(1)}, f32[96,192]{1,0:T(8,128)S(1)}, u32[]{:S(2)}, u32[]{:S(2)}) collective-permute-start(f32[96,192]{1,0:T(8,128)S(1)} %get-tuple-element.12), channel_id=1, source_target_pairs={{8,2},{5,15},{10,0},{7,13},{24,18},{21,31},{26,16},{23,29}} | collective-permute-start | bytes 221192 | tf_op jit(solution)/shard_map/ppermute | solution.py:39
  33.5 14.0 %collective-permute-start.7 = (f32[96,192]{1,0:T(8,128)S(1)}, f32[96,192]{1,0:T(8,128)S(1)}, u32[]{:S(2)}, u32[]{:S(2)}) collective-permute-start(f32[96,192]{1,0:T(8,128)S(1)} %get-tuple-element.15), channel_id=1, source_target_pairs={{8,12},{5,1},{10,14},{7,3},{24,28},{21,17},{26,30},{23,19}} | collective-permute-start | bytes 221192 | tf_op jit(solution)/shard_map/ppermute | solution.py:39
  34.2 13.4 %collective-permute-start.8 = (f32[96,192]{1,0:T(8,128)S(1)}, f32[96,192]{1,0:T(8,128)S(1)}, u32[]{:S(2)}, u32[]{:S(2)}) collective-permute-start(f32[96,192]{1,0:T(8,128)S(1)} %get-tuple-element.14), channel_id=1, source_target_pairs={{8,14},{5,3},{10,12},{7,1},{24,30},{21,19},{26,28},{23,17}} | collective-permute-start | bytes 221192 | tf_op jit(solution)/shard_map/ppermute | solution.py:39
  36.1 15.6 %collective-permute-start.10 = (f32[96,192]{1,0:T(8,128)S(1)}, f32[96,192]{1,0:T(8,128)S(1)}, u32[]{:S(2)}, u32[]{:S(2)}) collective-permute-start(f32[96,192]{1,0:T(8,128)S(1)} %get-tuple-element.16), channel_id=1, source_target_pairs={{0,7},{4,3},{8,2},{12,6},{13,10},{9,14},{5,15},{1,11},{2,5},{6,1},... | collective-permute-start | bytes 221192 | tf_op jit(solution)/shard_map/ppermute | solution.py:39
  45.4 6.4 %collective-permute-start.9 = (f32[96,192]{1,0:T(8,128)S(1)}, f32[96,192]{1,0:T(8,128)S(1)}, u32[]{:S(2)}, u32[]{:S(2)}) collective-permute-start(f32[96,192]{1,0:T(8,128)S(1)} %get-tuple-element.17), channel_id=1, source_target_pairs={{0,5},{4,1},{8,0},{12,4},{13,8},{9,12},{5,13},{1,9},{2,7},{6,3},{1... | collective-permute-start | bytes 221192 | tf_op jit(solution)/shard_map/ppermute | solution.py:39
  46.0 5.9 %collective-permute-start.11 = (f32[96,192]{1,0:T(8,128)S(1)}, f32[96,192]{1,0:T(8,128)S(1)}, u32[]{:S(2)}, u32[]{:S(2)}) collective-permute-start(f32[96,192]{1,0:T(8,128)S(1)} %dynamic-slice_bitcast_fusion.1), channel_id=1, source_target_pairs={{0,2},{4,6},{8,10},{12,14},{13,15},{9,11},{5,7},{1,3},{2,0},{6,4},... | collective-permute-start | bytes 221192 | tf_op jit(solution)/shard_map/ppermute | solution.py:39
  53.3 1.4 %collective-permute-start.14 = (f32[48,768]{1,0:T(8,128)S(1)}, f32[48,768]{1,0:T(8,128)S(1)}, u32[]{:S(2)}, u32[]{:S(2)}) collective-permute-start(f32[48,768]{1,0:T(8,128)S(1)} %dynamic-slice_bitcast_fusion), channel_id=1, source_target_pairs={{0,1},{1,0},{2,3},{3,2},{4,5},{5,4},{6,7},{7,6},{8,9},{9,8},{10,11... | collective-permute-start | bytes 442376 | tf_op jit(solution)/shard_map/ppermute | solution.py:91

commit v2 on v0

--- a/solution.py
+++ b/solution.py
@@ -3,7 +3,115 @@
 from jax import lax
 from jax.sharding import PartitionSpec as P
 
+
 PG = 4
+
+
+def dot(a, b):
+    return lax.dot_general(a, b, (((1,), (1,)), ((), ())), preferred_element_type=jnp.float32)
+
+
+def line(jacobian_tiles):
+    return body(jacobian_tiles)
+
+
+def body(jacobian_tiles):
+    own = jacobian_tiles[0]
+    width, cols = own.shape
+    n = lax.axis_size("walker") // PG
+    ring = 2 * n
+    quarter = width // PG
+    me = lax.axis_index("walker")
+    pos, group = me // PG, me % PG
+    side, core = group // 2, group % 2
+    group_index = jnp.where(core == 0, pos, n - 1 - pos)
+
+    def device(r, y):
+        r = r % ring
+        return r * PG + 2 * y if r < n else (ring - 1 - r) * PG + 2 * y + 1
+
+    def turn(to, flip=0, keep=lambda q: True):
+        return [
+            (device(r, y), device(to(r, r % n), y ^ flip))
+            for y in range(2)
+            for r in range(ring)
+            if keep(r % n)
+        ]
+
+    def move(value, pairs):
+        return lax.ppermute(value, "walker", pairs)
+
+    def pack(value):
+        return jnp.concatenate([value[:quarter], value[quarter:]], 1)
+
+    def unpack(value):
+        return jnp.concatenate([value[:, :width], value[:, width:]], 0)
+
+    def swap(value):
+        pairs = [(i, i ^ 1) for i in range(n * PG)]
+        return lax.ppermute(value, "walker", pairs)
+
+    k = cols // 2
+    own_parts = [own[:, :k], lax.optimization_barrier(own)[:, k:]]
+    a_parts = [move(part, turn(lambda r, q: r + 1)) for part in own_parts]
+    b_parts = [move(part, turn(lambda r, q: r + 1)) for part in a_parts]
+    p_parts = [swap(part) for part in b_parts]
+
+    def halves(block):
+        block = block.reshape(2, width // 2, width)
+        return (
+            lax.dynamic_index_in_dim(block, side, 0, False),
+            lax.dynamic_index_in_dim(block, 1 - side, 0, False),
+        )
+
+    s1 = dot(own, own)
+    s2, s2t = dot(own_parts[0], a_parts[0]), dot(a_parts[0], own_parts[0])
+    s2, s2t = lax.optimization_barrier((s2, s2t))
+    s2 += dot(own_parts[1], a_parts[1])
+    s2t += dot(a_parts[1], own_parts[1])
+    keep, send = zip(*(halves(s) for s in (s1, s2, s2t)))
+    early = jnp.stack(keep) + move(jnp.stack(send), turn(lambda r, q: r, 1))
+    early = lax.optimization_barrier(early)
+    up1 = move(early[2], turn(lambda r, q: r - 1))
+
+    s3, s3t = dot(own_parts[0], b_parts[0]), dot(b_parts[0], own_parts[0])
+    s3, s3t = lax.optimization_barrier((s3, s3t))
+    s3 += dot(own_parts[1], b_parts[1])
+    s3t += dot(b_parts[1], own_parts[1])
+    s4, s4t = dot(p_parts[0], b_parts[0]), dot(b_parts[0], p_parts[0])
+    s4, s4t = lax.optimization_barrier((s4, s4t))
+    s4 += dot(p_parts[1], b_parts[1])
+    s4t += dot(b_parts[1], p_parts[1])
+    lone = group_index == 1
+    far = jnp.where(lone, s4, s3t)
+    near = jnp.where(lone, s4t, s3)
+    far_keep, far_send = halves(far)
+    near_keep, near_send = halves(near)
+
+    route = {0: 6, 1: 3, 2: 0, 3: 1, 4: 2, 5: 7, 6: 4, 7: 5}
+    beside = {0: 1, 1: 0, 4: 5, 5: 4}
+    x = move(pack(far_keep), turn(lambda r, q: route[r]))
+    xf = move(pack(far_send), turn(lambda r, q: route[r], 1))
+    y = move(near_send, turn(lambda r, q: beside.get(r, r), 1))
+    z = move(near_keep, turn(lambda r, q: beside[r], keep=lambda q: q < 2))
+    x, xf, y, z, up1 = lax.optimization_barrier((x, xf, y, z, up1))
+    x = unpack(x + xf)
+    found = {0: early[0], -1: early[1], 1: up1, 2: x, -3: x, -2: near_keep + y, 3: z + y}
+    sign = 1 - 2 * core
+
+    def quarter_of(which):
+        blocks = []
+        for b in range(n):
+            offset = sign * (b - pos)
+            value = None
+            for d, v in found.items():
+                v = lax.dynamic_slice_in_dim(v, which * quarter, quarter, 0)
+                value = v if value is None else jnp.where(offset == d, v, value)
+            blocks.append(value)
+        return jnp.stack(blocks)
+
+    total = quarter_of(core) + swap(quarter_of(1 - core))
+    return jnp.concatenate([total[b] for b in range(n)], 1) / (cols * PG)
 
 
 def from_behind(block, axis, distance):
@@ -18,7 +126,7 @@
     return lax.ppermute(value, axis, pairs)
 
 
-def shards(jacobian_tiles):
+def long_line(jacobian_tiles):
     local_block = jacobian_tiles[0]
     blk_width = local_block.shape[0]
     params_all = local_block.shape[1] * PG
@@ -42,7 +150,7 @@
         tile_stack = lax.dynamic_update_index_in_dim(tile_stack, tile_with(moving), step_num, 0)
         return (moving, tile_stack)
 
-    unused_block, row_stack = lax.fori_loop(1, cycle_len, advance, (local_block, stack_init))
+    _, row_stack = lax.fori_loop(1, cycle_len, advance, (local_block, stack_init))
     for bit_num in range(PG.bit_length() - 2, -1, -1):
         half_rows = row_stack.shape[1] // 2
         my_bit = my_group >> bit_num & 1
@@ -54,9 +162,13 @@
     return gram_rows / params_all
 
 
+SPAN = 4
+
+
 def solution(mesh):
+    meets = mesh.shape["walker"] == SPAN * PG
     return jax.shard_map(
-        shards,
+        line if meets else long_line,
         mesh=mesh,
         in_specs=(P(("groups", "walker"), None, None),),
         out_specs=P(("groups", "walker"), None),

time: 76.2 us -> 47.4 us (0.62)
  waiting for transfers between devices: 56 us -> 20.3 us
  starting transfers between devices: 15.4 us -> 19.9 us
  other arithmetic: 0.13 us -> 1.41 us
  matrix products: 3 us -> 3.82 us
    ppermute x5 -> x13, waiting for transfers between devices: 56 us -> 20.3 us  [the longest x10 18.4 us: move(): return lax.ppermute(value, 'walker', pairs)]
    ppermute x5 -> x13, starting transfers between devices: 15.4 us -> 19.9 us  [the longest x10 19.8 us: move(): return lax.ppermute(value, 'walker', pairs)]
    slice x0 -> x4, local copies, waits for them, and re-layouts: none -> 1.22 us  [the longest x2 1.12 us: body(): own_parts = [own[:, :k], lax.optimization_barrier(own)[:, k:]]]
    div x2 -> x0, local copies, waits for them, and re-layouts: 0.93 us -> none  [shards(): return gram_rows / params_all]
    dot_general x4 -> x13, matrix products: 3 us -> 3.82 us  [dot(): lax.dot_general(a, b, (((1,), (1,)), ((), ())), preferred_element_type=jn...]
  transfers between devices with their start and end apart: 5 -> 13, of which waited for: 5 -> 9; matrix products, arithmetic and copies ran while one was open for 0% -> 8% of each run, Pallas kernels for 0% -> 0%
where the time goes in v2:
time: 47.4 us; the launch traced here: 47.2 us
  waiting for transfers between devices  20.3 us (43%)
  starting transfers between devices  19.9 us (42%)
  matrix products  3.82 us (8%)
  other arithmetic  1.41 us (3%)
  local copies, waits for them, and re-layouts  1.34 us (3%)
    ppermute x10, starting transfers between devices, move(): return lax.ppermute(value, 'walker', pairs)  19.8 us
    ppermute x10, waiting for transfers between devices, move(): return lax.ppermute(value, 'walker', pairs)  18.4 us
    dot_general x13, matrix products, dot(): lax.dot_general(a, b, (((1,), (1,)), ((), ())), preferred_element_type=jn...  3.82 us
    ppermute x3, waiting for transfers between devices, swap(): return lax.ppermute(value, 'walker', pairs)  1.92 us
    slice x2, local copies, waits for them, and re-layouts, body(): own_parts = [own[:, :k], lax.optimization_barrier(own)[:, k:]]  1.12 us
  transfers between devices with their start and end apart: 13, of which 9 were waited for; matrix products, arithmetic and copies ran while one was open for 8% of the time, Pallas kernels for 0%

profile of v2, /device:TPU:0, one launch (start us, length us, event | category | flops | bytes accessed | tf_op | source)
XLA Modules:
  0.0 47.2 jit_solution(4491181632710391716)
XLA Ops:
  0.0 0.0 copy-start
  0.0 1.1 %slice.76 = bf16[192,1024]{1,0:T(8,128)(2,1)S(1)} slice(bf16[192,2048]{1,0:T(8,128)(2,1)} %bitcast.96), slice={[0:192], [0:1024]} | slice | bytes 786432 | tf_op jit(solution)/shard_map/slice | solution.py:55
  1.1 3.1 %collective-permute-start = (bf16[192,1024]{1,0:T(8,128)(2,1)S(1)}, bf16[192,1024]{1,0:T(8,128)(2,1)S(1)}, u32[]{:S(2)}, u32[]{:S(2)}) collective-permute-start(bf16[192,1024]{1,0:T(8,128)(2,1)S(1)} %slice.76), channel_id=1, source_target_pairs={{0,4},{4,8},{8,12},{12,13},{13,9},{9,5},{5,1},{1,0},{2,6},{6,10},{... | collective-permute-start | bytes 1179656 | tf_op jit(solution)/shard_map/ppermute | solution.py:42
  4.2 0.0 copy-done
  4.2 1.6 %collective-permute-start.3 = (bf16[192,1024]{1,0:T(8,128)(2,1)S(1)}, bf16[192,1024]{1,0:T(8,128)(2,1)S(1)}, u32[]{:S(2)}, u32[]{:S(2)}) collective-permute-start(bf16[192,1024]{1,0:T(8,128)(2,1)S(1)} %slice.77), channel_id=1, source_target_pairs={{0,4},{4,8},{8,12},{12,13},{13,9},{9,5},{5,1},{1,0},{2,6},{6,10},{... | collective-permute-start | bytes 1179656 | tf_op jit(solution)/shard_map/ppermute | solution.py:42
  5.8 0.4 fusion
  6.2 3.2 %collective-permute-done = bf16[192,1024]{1,0:T(8,128)(2,1)S(1)} collective-permute-done((bf16[192,1024]{1,0:T(8,128)(2,1)S(1)}, bf16[192,1024]{1,0:T(8,128)(2,1)S(1)}, u32[]{:S(2)}, u32[]{:S(2)}) %collective-permute-start) | collective-permute-done | bytes 393248 | tf_op jit(solution)/shard_map/ppermute | solution.py:42
  9.5 0.3 fusion.38
  9.8 0.3 fusion.36
  10.1 3.6 %collective-permute-done.3 = bf16[192,1024]{1,0:T(8,128)(2,1)S(1)} collective-permute-done((bf16[192,1024]{1,0:T(8,128)(2,1)S(1)}, bf16[192,1024]{1,0:T(8,128)(2,1)S(1)}, u32[]{:S(2)}, u32[]{:S(2)}) %collective-permute-start.3) | collective-permute-done | bytes 393248 | tf_op jit(solution)/shard_map/ppermute | solution.py:42
  13.7 0.3 fusion.28
  14.0 0.3 fusion.30
  14.4 1.6 %collective-permute-start.10 = (f32[3,96,192]{2,1,0:T(8,128)S(1)}, f32[3,96,192]{2,1,0:T(8,128)S(1)}, u32[]{:S(2)}, u32[]{:S(2)}) collective-permute-start(f32[3,96,192]{2,1,0:T(8,128)S(1)} %pad_maximum_fusion), channel_id=1, source_target_pairs={{0,2},{4,6},{8,10},{12,14},{13,15},{9,11},{5,7},{1,3},{2,0},{6,4},... | collective-permute-start | bytes 663560 | tf_op jit(solution)/shard_map/ppermute | solution.py:42
  16.0 2.5 %collective-permute-start.1 = (bf16[192,1024]{1,0:T(8,128)(2,1)S(1)}, bf16[192,1024]{1,0:T(8,128)(2,1)S(1)}, u32[]{:S(2)}, u32[]{:S(2)}) collective-permute-start(bf16[192,1024]{1,0:T(8,128)(2,1)S(1)} %collective-permute-done), channel_id=1, source_target_pairs={{0,4},{4,8},{8,12},{12,13},{13,9},{9,5},{5,1},{1,0},{2,6},{6,10},{... | collective-permute-start | bytes 1179656 | tf_op jit(solution)/shard_map/ppermute | solution.py:42
  18.5 1.6 %collective-permute-start.4 = (bf16[192,1024]{1,0:T(8,128)(2,1)S(1)}, bf16[192,1024]{1,0:T(8,128)(2,1)S(1)}, u32[]{:S(2)}, u32[]{:S(2)}) collective-permute-start(bf16[192,1024]{1,0:T(8,128)(2,1)S(1)} %collective-permute-done.3), channel_id=1, source_target_pairs={{0,4},{4,8},{8,12},{12,13},{13,9},{9,5},{5,1},{1,0},{2,6},{6,10},{... | collective-permute-start | bytes 1179656 | tf_op jit(solution)/shard_map/ppermute | solution.py:42
  20.1 2.8 %collective-permute-done.10 = f32[3,96,192]{2,1,0:T(8,128)S(1)} collective-permute-done((f32[3,96,192]{2,1,0:T(8,128)S(1)}, f32[3,96,192]{2,1,0:T(8,128)S(1)}, u32[]{:S(2)}, u32[]{:S(2)}) %collective-permute-start.10) | collective-permute-done | bytes 221216 | tf_op jit(solution)/shard_map/ppermute | solution.py:42
  22.9 0.0 collective-permute-start.11
  22.9 1.4 %collective-permute-done.1 = bf16[192,1024]{1,0:T(8,128)(2,1)S(1)} collective-permute-done((bf16[192,1024]{1,0:T(8,128)(2,1)S(1)}, bf16[192,1024]{1,0:T(8,128)(2,1)S(1)}, u32[]{:S(2)}, u32[]{:S(2)}) %collective-permute-start.1) | collective-permute-done | bytes 393248 | tf_op jit(solution)/shard_map/ppermute | solution.py:42
  24.4 0.3 fusion.42
  24.7 0.3 fusion.40
  24.9 0.1 collective-permute-start.2
  25.0 4.0 %collective-permute-done.4 = bf16[192,1024]{1,0:T(8,128)(2,1)S(1)} collective-permute-done((bf16[192,1024]{1,0:T(8,128)(2,1)S(1)}, bf16[192,1024]{1,0:T(8,128)(2,1)S(1)}, u32[]{:S(2)}, u32[]{:S(2)}) %collective-permute-start.4) | collective-permute-done | bytes 393248 | tf_op jit(solution)/shard_map/ppermute | solution.py:42
  29.0 0.0 collective-permute-start.5
  29.0 0.3 fusion.32
  29.3 0.3 fusion.34
  29.6 0.0 collective-permute-done.2
  29.6 0.3 fusion.48
  29.9 0.3 fusion.49
  30.2 0.5 %collective-permute-done.5 = bf16[192,1024]{1,0:T(8,128)(2,1)S(1)} collective-permute-done((bf16[192,1024]{1,0:T(8,128)(2,1)S(1)}, bf16[192,1024]{1,0:T(8,128)(2,1)S(1)}, u32[]{:S(2)}, u32[]{:S(2)}) %collective-permute-start.5) | collective-permute-done | bytes 393248 | tf_op jit(solution)/shard_map/ppermute | solution.py:52
  30.8 0.3 fusion.51
  31.1 0.3 fusion.50
  31.3 0.1 add_select_fusion
  31.5 0.1 pad_maximum_fusion.2
  31.6 2.2 %collective-permute-start.6 = (f32[48,384]{1,0:T(8,128)S(1)}, f32[48,384]{1,0:T(8,128)S(1)}, u32[]{:S(2)}, u32[]{:S(2)}) collective-permute-start(f32[48,384]{1,0:T(8,128)S(1)} %pad_maximum_fusion.2), channel_id=1, source_target_pairs={{0,5},{4,12},{8,0},{12,4},{13,8},{9,1},{5,13},{1,9},{2,7},{6,14},{... | collective-permute-start | bytes 221192 | tf_op jit(solution)/shard_map/ppermute | solution.py:42
  33.8 0.1 pad_maximum_fusion.3
  33.9 2.3 %collective-permute-start.7 = (f32[48,384]{1,0:T(8,128)S(1)}, f32[48,384]{1,0:T(8,128)S(1)}, u32[]{:S(2)}, u32[]{:S(2)}) collective-permute-start(f32[48,384]{1,0:T(8,128)S(1)} %pad_maximum_fusion.3), channel_id=1, source_target_pairs={{0,7},{4,14},{8,2},{12,6},{13,10},{9,3},{5,15},{1,11},{2,5},{6,12}... | collective-permute-start | bytes 221192 | tf_op jit(solution)/shard_map/ppermute | solution.py:42
  36.2 1.9 %collective-permute-start.8 = (f32[96,192]{1,0:T(8,128)S(1)}, f32[96,192]{1,0:T(8,128)S(1)}, u32[]{:S(2)}, u32[]{:S(2)}) collective-permute-start(f32[96,192]{1,0:T(8,128)S(1)} %get-tuple-element.47), channel_id=1, source_target_pairs={{0,6},{4,2},{8,10},{12,14},{13,11},{9,15},{5,7},{1,3},{2,4},{6,0},... | collective-permute-start | bytes 221192 | tf_op jit(solution)/shard_map/ppermute | solution.py:42
  38.1 3.1 %collective-permute-start.9 = (f32[96,192]{1,0:T(8,128)S(1)}, f32[96,192]{1,0:T(8,128)S(1)}, u32[]{:S(2)}, u32[]{:S(2)}) collective-permute-start(f32[96,192]{1,0:T(8,128)S(1)} %get-tuple-element.46), channel_id=1, source_target_pairs={{0,4},{4,0},{13,9},{9,13},{2,6},{6,2},{15,11},{11,15},{16,20},{20,... | collective-permute-start | bytes 221192 | tf_op jit(solution)/shard_map/ppermute | solution.py:42
  41.2 0.0 collective-permute-done.11
  41.2 0.0 collective-permute-done.6
  41.2 0.0 collective-permute-done.7
  41.2 0.8 %collective-permute-done.8 = f32[96,192]{1,0:T(8,128)S(1)} collective-permute-done((f32[96,192]{1,0:T(8,128)S(1)}, f32[96,192]{1,0:T(8,128)S(1)}, u32[]{:S(2)}, u32[]{:S(2)}) %collective-permute-start.8) | collective-permute-done | bytes 73760 | tf_op jit(solution)/shard_map/ppermute | solution.py:42
  42.0 2.6 %collective-permute-done.9 = f32[96,192]{1,0:T(8,128)S(1)} collective-permute-done((f32[96,192]{1,0:T(8,128)S(1)}, f32[96,192]{1,0:T(8,128)S(1)}, u32[]{:S(2)}, u32[]{:S(2)}) %collective-permute-start.9) | collective-permute-done | bytes 73760 | tf_op jit(solution)/shard_map/ppermute | solution.py:42
  44.6 0.1 fusion.47
  44.7 0.1 fusion.4
  44.8 0.1 fusion.13
  44.9 0.1 collective-permute-start.12
  45.0 1.4 %collective-permute-done.12 = f32[4,48,192]{2,1,0:T(8,128)S(1)} collective-permute-done((f32[4,48,192]{2,1,0:T(8,128)S(1)}, f32[4,48,192]{2,1,0:T(8,128)S(1)}, u32[]{:S(2)}, u32[]{:S(2)}) %collective-permute-start.12) | collective-permute-done | bytes 147488 | tf_op jit(solution)/shard_map/ppermute | solution.py:52
  46.4 0.8 %maximum_multiply_fusion = f32[48,768]{1,0:T(8,128)} fusion(f32[48,192]{1,0:T(8,128)S(1)} %get-tuple-element.43, f32[48,192]{1,0:T(8,128)S(1)} %get-tuple-element.44, f32[48,192]{1,0:T(8,128)S(1)} %get-tuple-element.45, f32[48,192]{1,0:T(8,128)S(1)} %get-tuple-element.42), kind=kLoop, calls=%fused_computation.8 | loop fusion | flops 147456 | bytes 294912 | tf_op jit(solution)/shard_map/div | solution.py:114
  (17 shorter events, 0.4 us)
Async XLA Ops:
  0.0 4.2 %copy-start = (bf16[1,192,2048]{2,1,0:T(8,128)(2,1)S(1)}, bf16[1,192,2048]{2,1,0:T(8,128)(2,1)}, u32[]{:S(2)}) copy-start(bf16[1,192,2048]{2,1,0:T(8,128)(2,1)} %param.1) | copy-start | bytes 2359300
  1.1 8.4 %collective-permute-start = (bf16[192,1024]{1,0:T(8,128)(2,1)S(1)}, bf16[192,1024]{1,0:T(8,128)(2,1)S(1)}, u32[]{:S(2)}, u32[]{:S(2)}) collective-permute-start(bf16[192,1024]{1,0:T(8,128)(2,1)S(1)} %slice.76), channel_id=1, source_target_pairs={{0,4},{4,8},{8,12},{12,13},{13,9},{9,5},{5,1},{1,0},{2,6},{6,10},{... | collective-permute-start | bytes 1179656 | tf_op jit(solution)/shard_map/ppermute | solution.py:42
  4.2 9.5 %collective-permute-start.3 = (bf16[192,1024]{1,0:T(8,128)(2,1)S(1)}, bf16[192,1024]{1,0:T(8,128)(2,1)S(1)}, u32[]{:S(2)}, u32[]{:S(2)}) collective-permute-start(bf16[192,1024]{1,0:T(8,128)(2,1)S(1)} %slice.77), channel_id=1, source_target_pairs={{0,4},{4,8},{8,12},{12,13},{13,9},{9,5},{5,1},{1,0},{2,6},{6,10},{... | collective-permute-start | bytes 1179656 | tf_op jit(solution)/shard_map/ppermute | solution.py:42
  14.4 8.4 %collective-permute-start.10 = (f32[3,96,192]{2,1,0:T(8,128)S(1)}, f32[3,96,192]{2,1,0:T(8,128)S(1)}, u32[]{:S(2)}, u32[]{:S(2)}) collective-permute-start(f32[3,96,192]{2,1,0:T(8,128)S(1)} %pad_maximum_fusion), channel_id=1, source_target_pairs={{0,2},{4,6},{8,10},{12,14},{13,15},{9,11},{5,7},{1,3},{2,0},{6,4},... | collective-permute-start | bytes 663560 | tf_op jit(solution)/shard_map/ppermute | solution.py:42
  16.0 8.4 %collective-permute-start.1 = (bf16[192,1024]{1,0:T(8,128)(2,1)S(1)}, bf16[192,1024]{1,0:T(8,128)(2,1)S(1)}, u32[]{:S(2)}, u32[]{:S(2)}) collective-permute-start(bf16[192,1024]{1,0:T(8,128)(2,1)S(1)} %collective-permute-done), channel_id=1, source_target_pairs={{0,4},{4,8},{8,12},{12,13},{13,9},{9,5},{5,1},{1,0},{2,6},{6,10},{... | collective-permute-start | bytes 1179656 | tf_op jit(solution)/shard_map/ppermute | solution.py:42
  18.5 10.6 %collective-permute-start.4 = (bf16[192,1024]{1,0:T(8,128)(2,1)S(1)}, bf16[192,1024]{1,0:T(8,128)(2,1)S(1)}, u32[]{:S(2)}, u32[]{:S(2)}) collective-permute-start(bf16[192,1024]{1,0:T(8,128)(2,1)S(1)} %collective-permute-done.3), channel_id=1, source_target_pairs={{0,4},{4,8},{8,12},{12,13},{13,9},{9,5},{5,1},{1,0},{2,6},{6,10},{... | collective-permute-start | bytes 1179656 | tf_op jit(solution)/shard_map/ppermute | solution.py:42
  22.9 18.3 %collective-permute-start.11 = (f32[96,192]{1,0:T(8,128)S(1)}, f32[96,192]{1,0:T(8,128)S(1)}, u32[]{:S(2)}, u32[]{:S(2)}) collective-permute-start(f32[96,192]{1,0:T(8,128)S(1)} %get-tuple-element.39), channel_id=1, source_target_pairs={{0,1},{4,0},{8,4},{12,8},{13,12},{9,13},{5,9},{1,5},{2,3},{6,2},{1... | collective-permute-start | bytes 221192 | tf_op jit(solution)/shard_map/ppermute | solution.py:42
  24.9 4.7 %collective-permute-start.2 = (bf16[192,1024]{1,0:T(8,128)(2,1)S(1)}, bf16[192,1024]{1,0:T(8,128)(2,1)S(1)}, u32[]{:S(2)}, u32[]{:S(2)}) collective-permute-start(bf16[192,1024]{1,0:T(8,128)(2,1)S(1)} %collective-permute-done.1), channel_id=1, source_target_pairs={{0,1},{1,0},{2,3},{3,2},{4,5},{5,4},{6,7},{7,6},{8,9},{9,8},{10,11... | collective-permute-start | bytes 1179656 | tf_op jit(solution)/shard_map/ppermute | solution.py:52
  29.0 1.7 %collective-permute-start.5 = (bf16[192,1024]{1,0:T(8,128)(2,1)S(1)}, bf16[192,1024]{1,0:T(8,128)(2,1)S(1)}, u32[]{:S(2)}, u32[]{:S(2)}) collective-permute-start(bf16[192,1024]{1,0:T(8,128)(2,1)S(1)} %collective-permute-done.4), channel_id=1, source_target_pairs={{0,1},{1,0},{2,3},{3,2},{4,5},{5,4},{6,7},{7,6},{8,9},{9,8},{10,11... | collective-permute-start | bytes 1179656 | tf_op jit(solution)/shard_map/ppermute | solution.py:52
  31.6 9.6 %collective-permute-start.6 = (f32[48,384]{1,0:T(8,128)S(1)}, f32[48,384]{1,0:T(8,128)S(1)}, u32[]{:S(2)}, u32[]{:S(2)}) collective-permute-start(f32[48,384]{1,0:T(8,128)S(1)} %pad_maximum_fusion.2), channel_id=1, source_target_pairs={{0,5},{4,12},{8,0},{12,4},{13,8},{9,1},{5,13},{1,9},{2,7},{6,14},{... | collective-permute-start | bytes 221192 | tf_op jit(solution)/shard_map/ppermute | solution.py:42
  33.9 7.3 %collective-permute-start.7 = (f32[48,384]{1,0:T(8,128)S(1)}, f32[48,384]{1,0:T(8,128)S(1)}, u32[]{:S(2)}, u32[]{:S(2)}) collective-permute-start(f32[48,384]{1,0:T(8,128)S(1)} %pad_maximum_fusion.3), channel_id=1, source_target_pairs={{0,7},{4,14},{8,2},{12,6},{13,10},{9,3},{5,15},{1,11},{2,5},{6,12}... | collective-permute-start | bytes 221192 | tf_op jit(solution)/shard_map/ppermute | solution.py:42
  36.2 5.8 %collective-permute-start.8 = (f32[96,192]{1,0:T(8,128)S(1)}, f32[96,192]{1,0:T(8,128)S(1)}, u32[]{:S(2)}, u32[]{:S(2)}) collective-permute-start(f32[96,192]{1,0:T(8,128)S(1)} %get-tuple-element.47), channel_id=1, source_target_pairs={{0,6},{4,2},{8,10},{12,14},{13,11},{9,15},{5,7},{1,3},{2,4},{6,0},... | collective-permute-start | bytes 221192 | tf_op jit(solution)/shard_map/ppermute | solution.py:42
  38.1 6.5 %collective-permute-start.9 = (f32[96,192]{1,0:T(8,128)S(1)}, f32[96,192]{1,0:T(8,128)S(1)}, u32[]{:S(2)}, u32[]{:S(2)}) collective-permute-start(f32[96,192]{1,0:T(8,128)S(1)} %get-tuple-element.46), channel_id=1, source_target_pairs={{0,4},{4,0},{13,9},{9,13},{2,6},{6,2},{15,11},{11,15},{16,20},{20,... | collective-permute-start | bytes 221192 | tf_op jit(solution)/shard_map/ppermute | solution.py:42
  44.9 1.5 %collective-permute-start.12 = (f32[4,48,192]{2,1,0:T(8,128)S(1)}, f32[4,48,192]{2,1,0:T(8,128)S(1)}, u32[]{:S(2)}, u32[]{:S(2)}) collective-permute-start(f32[4,48,192]{2,1,0:T(8,128)S(1)} %pad_maximum_fusion.1), channel_id=1, source_target_pairs={{0,1},{1,0},{2,3},{3,2},{4,5},{5,4},{6,7},{7,6},{8,9},{9,8},{10,11... | collective-permute-start | bytes 442376 | tf_op jit(solution)/shard_map/ppermute | solution.py:52

commit v3 on v2

--- a/solution.py
+++ b/solution.py
@@ -51,11 +51,23 @@
         pairs = [(i, i ^ 1) for i in range(n * PG)]
         return lax.ppermute(value, "walker", pairs)
 
-    k = cols // 2
-    own_parts = [own[:, :k], lax.optimization_barrier(own)[:, k:]]
+    edges = [cols * c // CUTS[-1] for c in (0, *CUTS)]
+    spans = list(zip(edges, edges[1:]))
+    own_parts = [own[:, spans[0][0] : spans[0][1]]]
+    rest = lax.optimization_barrier(own)
+    own_parts += [rest[:, lo:hi] for lo, hi in spans[1:]]
     a_parts = [move(part, turn(lambda r, q: r + 1)) for part in own_parts]
     b_parts = [move(part, turn(lambda r, q: r + 1)) for part in a_parts]
     p_parts = [swap(part) for part in b_parts]
+
+    def products(xs, ys):
+        forth, back = 0.0, 0.0
+        for i, (x, y) in enumerate(zip(xs, ys)):
+            forth += dot(x, y)
+            back += dot(y, x)
+            if i + 1 < len(xs):
+                forth, back = lax.optimization_barrier((forth, back))
+        return forth, back
 
     def halves(block):
         block = block.reshape(2, width // 2, width)
@@ -65,23 +77,13 @@
         )
 
     s1 = dot(own, own)
-    s2, s2t = dot(own_parts[0], a_parts[0]), dot(a_parts[0], own_parts[0])
-    s2, s2t = lax.optimization_barrier((s2, s2t))
-    s2 += dot(own_parts[1], a_parts[1])
-    s2t += dot(a_parts[1], own_parts[1])
+    s2, s2t = products(own_parts, a_parts)
     keep, send = zip(*(halves(s) for s in (s1, s2, s2t)))
     early = jnp.stack(keep) + move(jnp.stack(send), turn(lambda r, q: r, 1))
     early = lax.optimization_barrier(early)
-    up1 = move(early[2], turn(lambda r, q: r - 1))
 
-    s3, s3t = dot(own_parts[0], b_parts[0]), dot(b_parts[0], own_parts[0])
-    s3, s3t = lax.optimization_barrier((s3, s3t))
-    s3 += dot(own_parts[1], b_parts[1])
-    s3t += dot(b_parts[1], own_parts[1])
-    s4, s4t = dot(p_parts[0], b_parts[0]), dot(b_parts[0], p_parts[0])
-    s4, s4t = lax.optimization_barrier((s4, s4t))
-    s4 += dot(p_parts[1], b_parts[1])
-    s4t += dot(b_parts[1], p_parts[1])
+    s3, s3t = products(own_parts, b_parts)
+    s4, s4t = products(p_parts, b_parts)
     lone = group_index == 1
     far = jnp.where(lone, s4, s3t)
     near = jnp.where(lone, s4t, s3)
@@ -92,10 +94,12 @@
     beside = {0: 1, 1: 0, 4: 5, 5: 4}
     x = move(pack(far_keep), turn(lambda r, q: route[r]))
     xf = move(pack(far_send), turn(lambda r, q: route[r], 1))
-    y = move(near_send, turn(lambda r, q: beside.get(r, r), 1))
-    z = move(near_keep, turn(lambda r, q: beside[r], keep=lambda q: q < 2))
-    x, xf, y, z, up1 = lax.optimization_barrier((x, xf, y, z, up1))
+    y = move(pack(near_send), turn(lambda r, q: beside.get(r, r), 1))
+    ez = move(jnp.concatenate([early[2], near_keep], 1), turn(lambda r, q: r - 1))
+    x, xf, y, ez = lax.optimization_barrier((x, xf, y, ez))
     x = unpack(x + xf)
+    y = unpack(y)
+    up1, z = ez[:, :width], ez[:, width:]
     found = {0: early[0], -1: early[1], 1: up1, 2: x, -3: x, -2: near_keep + y, 3: z + y}
     sign = 1 - 2 * core
 
@@ -163,6 +167,7 @@
 
 
 SPAN = 4
+CUTS = (3, 6, 8)
 
 
 def solution(mesh):

time: 47.4 us -> 46.5 us (0.981)
  waiting for transfers between devices: 20.3 us -> 16.7 us
  local copies, waits for them, and re-layouts: 1.34 us -> 2.36 us
  matrix products: 3.82 us -> 4.82 us
    ppermute x10 -> x11, waiting for transfers between devices: 18.4 us -> 14.5 us  [move(): return lax.ppermute(value, 'walker', pairs)]
    dot_general x13 -> x19, matrix products: 3.82 us -> 4.82 us  [dot(): lax.dot_general(a, b, (((1,), (1,)), ((), ())), preferred_element_type=jn...]
    slice x2 -> x3, local copies, waits for them, and re-layouts: 1.12 us -> 2.05 us  [the longest x1 1.05 us: body(): own_parts = [own[:, spans[0][0]:spans[0][1]]]]
    ppermute x3 -> x4, waiting for transfers between devices: 1.92 us -> 2.19 us  [swap(): return lax.ppermute(value, 'walker', pairs)]
    ppermute x10 -> x11, starting transfers between devices: 19.8 us -> 19.9 us  [move(): return lax.ppermute(value, 'walker', pairs)]
  transfers between devices with their start and end apart: 13 -> 15, of which waited for: 9 -> 8; matrix products, arithmetic and copies ran while one was open for 8% -> 13% of each run, Pallas kernels for 0% -> 0%
where the time goes in v3:
time: 46.5 us; the launch traced here: 46.4 us
  starting transfers between devices  20.2 us (43%)
  waiting for transfers between devices  16.7 us (36%)
  matrix products  4.82 us (10%)
  local copies, waits for them, and re-layouts  2.36 us (5%)
  other arithmetic  1.83 us (4%)
  between operations  0.47 us (1%)
    ppermute x11, starting transfers between devices, move(): return lax.ppermute(value, 'walker', pairs)  19.9 us
    ppermute x11, waiting for transfers between devices, move(): return lax.ppermute(value, 'walker', pairs)  14.5 us
    dot_general x19, matrix products, dot(): lax.dot_general(a, b, (((1,), (1,)), ((), ())), preferred_element_type=jn...  4.82 us
    ppermute x4, waiting for transfers between devices, swap(): return lax.ppermute(value, 'walker', pairs)  2.19 us
    slice x1, local copies, waits for them, and re-layouts, body(): own_parts = [own[:, spans[0][0]:spans[0][1]]]  1.05 us
    slice x2, local copies, waits for them, and re-layouts, body(): own_parts += [rest[:, lo:hi] for lo, hi in spans[1:]]  0.99 us
  transfers between devices with their start and end apart: 15, of which 8 were waited for; matrix products, arithmetic and copies ran while one was open for 13% of the time, Pallas kernels for 0%

profile of v3, /device:TPU:0, one launch (start us, length us, event | category | flops | bytes accessed | tf_op | source)
XLA Modules:
  0.0 46.4 jit_solution(6113202120932118933)
XLA Ops:
  0.0 0.0 copy-start
  0.0 1.1 %slice.112 = bf16[192,768]{1,0:T(8,128)(2,1)S(1)} slice(bf16[192,2048]{1,0:T(8,128)(2,1)} %bitcast.108), slice={[0:192], [0:768]} | slice | bytes 589824 | tf_op jit(solution)/shard_map/slice | solution.py:56
  1.1 3.1 %collective-permute-start = (bf16[192,768]{1,0:T(8,128)(2,1)S(1)}, bf16[192,768]{1,0:T(8,128)(2,1)S(1)}, u32[]{:S(2)}, u32[]{:S(2)}) collective-permute-start(bf16[192,768]{1,0:T(8,128)(2,1)S(1)} %slice.112), channel_id=1, source_target_pairs={{0,4},{4,8},{8,12},{12,13},{13,9},{9,5},{5,1},{1,0},{2,6},{6,10},{... | collective-permute-start | bytes 884744 | tf_op jit(solution)/shard_map/ppermute | solution.py:42
  4.1 1.0 %slice.113 = bf16[192,768]{1,0:T(8,128)(2,1)S(1)} slice(bf16[192,2048]{1,0:T(8,128)(2,1)} %bitcast.109), slice={[0:192], [768:1536]} | slice | bytes 589824 | tf_op jit(solution)/shard_map/slice | solution.py:58
  5.1 1.6 %collective-permute-start.3 = (bf16[192,768]{1,0:T(8,128)(2,1)S(1)}, bf16[192,768]{1,0:T(8,128)(2,1)S(1)}, u32[]{:S(2)}, u32[]{:S(2)}) collective-permute-start(bf16[192,768]{1,0:T(8,128)(2,1)S(1)} %slice.113), channel_id=1, source_target_pairs={{0,4},{4,8},{8,12},{12,13},{13,9},{9,5},{5,1},{1,0},{2,6},{6,10},{... | collective-permute-start | bytes 884744 | tf_op jit(solution)/shard_map/ppermute | solution.py:42
  6.7 0.0 copy-done
  6.7 1.6 %collective-permute-start.6 = (bf16[192,512]{1,0:T(8,128)(2,1)S(1)}, bf16[192,512]{1,0:T(8,128)(2,1)S(1)}, u32[]{:S(2)}, u32[]{:S(2)}) collective-permute-start(bf16[192,512]{1,0:T(8,128)(2,1)S(1)} %slice.114), channel_id=1, source_target_pairs={{0,4},{4,8},{8,12},{12,13},{13,9},{9,5},{5,1},{1,0},{2,6},{6,10},{... | collective-permute-start | bytes 589832 | tf_op jit(solution)/shard_map/ppermute | solution.py:42
  8.3 0.4 fusion
  8.8 4.8 %collective-permute-done.6 = bf16[192,512]{1,0:T(8,128)(2,1)S(1)} collective-permute-done((bf16[192,512]{1,0:T(8,128)(2,1)S(1)}, bf16[192,512]{1,0:T(8,128)(2,1)S(1)}, u32[]{:S(2)}, u32[]{:S(2)}) %collective-permute-start.6) | collective-permute-done | bytes 196640 | tf_op jit(solution)/shard_map/ppermute | solution.py:42
  13.6 0.2 fusion.29
  13.9 2.5 %collective-permute-start.7 = (bf16[192,512]{1,0:T(8,128)(2,1)S(1)}, bf16[192,512]{1,0:T(8,128)(2,1)S(1)}, u32[]{:S(2)}, u32[]{:S(2)}) collective-permute-start(bf16[192,512]{1,0:T(8,128)(2,1)S(1)} %collective-permute-done.6), channel_id=1, source_target_pairs={{0,4},{4,8},{8,12},{12,13},{13,9},{9,5},{5,1},{1,0},{2,6},{6,10},{... | collective-permute-start | bytes 589832 | tf_op jit(solution)/shard_map/ppermute | solution.py:42
  16.4 0.2 fusion.31
  16.6 0.0 collective-permute-done
  16.6 0.3 fusion.47
  16.9 0.3 fusion.45
  17.1 0.0 collective-permute-done.3
  17.2 0.3 fusion.39
  17.5 0.3 fusion.37
  17.9 1.6 %collective-permute-start.12 = (f32[3,96,192]{2,1,0:T(8,128)S(1)}, f32[3,96,192]{2,1,0:T(8,128)S(1)}, u32[]{:S(2)}, u32[]{:S(2)}) collective-permute-start(f32[3,96,192]{2,1,0:T(8,128)S(1)} %pad_maximum_fusion), channel_id=1, source_target_pairs={{0,2},{4,6},{8,10},{12,14},{13,15},{9,11},{5,7},{1,3},{2,0},{6,4},... | collective-permute-start | bytes 663560 | tf_op jit(solution)/shard_map/ppermute | solution.py:42
  19.5 1.6 %collective-permute-start.1 = (bf16[192,768]{1,0:T(8,128)(2,1)S(1)}, bf16[192,768]{1,0:T(8,128)(2,1)S(1)}, u32[]{:S(2)}, u32[]{:S(2)}) collective-permute-start(bf16[192,768]{1,0:T(8,128)(2,1)S(1)} %collective-permute-done), channel_id=1, source_target_pairs={{0,4},{4,8},{8,12},{12,13},{13,9},{9,5},{5,1},{1,0},{2,6},{6,10},{... | collective-permute-start | bytes 884744 | tf_op jit(solution)/shard_map/ppermute | solution.py:42
  21.1 1.6 %collective-permute-start.4 = (bf16[192,768]{1,0:T(8,128)(2,1)S(1)}, bf16[192,768]{1,0:T(8,128)(2,1)S(1)}, u32[]{:S(2)}, u32[]{:S(2)}) collective-permute-start(bf16[192,768]{1,0:T(8,128)(2,1)S(1)} %collective-permute-done.3), channel_id=1, source_target_pairs={{0,4},{4,8},{8,12},{12,13},{13,9},{9,5},{5,1},{1,0},{2,6},{6,10},{... | collective-permute-start | bytes 884744 | tf_op jit(solution)/shard_map/ppermute | solution.py:42
  22.6 0.0 collective-permute-done.7
  22.6 0.2 fusion.33
  22.9 0.1 collective-permute-start.8
  22.9 0.2 fusion.35
  23.2 1.7 %collective-permute-done.12 = f32[3,96,192]{2,1,0:T(8,128)S(1)} collective-permute-done((f32[3,96,192]{2,1,0:T(8,128)S(1)}, f32[3,96,192]{2,1,0:T(8,128)S(1)}, u32[]{:S(2)}, u32[]{:S(2)}) %collective-permute-start.12) | collective-permute-done | bytes 221216 | tf_op jit(solution)/shard_map/ppermute | solution.py:42
  25.0 0.3 collective-permute-done.1
  25.3 0.3 fusion.51
  25.6 0.1 collective-permute-start.2
  25.6 0.3 fusion.49
  25.9 2.5 %collective-permute-done.4 = bf16[192,768]{1,0:T(8,128)(2,1)S(1)} collective-permute-done((bf16[192,768]{1,0:T(8,128)(2,1)S(1)}, bf16[192,768]{1,0:T(8,128)(2,1)S(1)}, u32[]{:S(2)}, u32[]{:S(2)}) %collective-permute-start.4) | collective-permute-done | bytes 294944 | tf_op jit(solution)/shard_map/ppermute | solution.py:42
  28.5 0.3 fusion.43
  28.7 0.3 fusion.41
  29.0 0.0 collective-permute-done.8
  29.0 0.2 fusion.62
  29.3 0.1 collective-permute-start.5
  29.4 0.2 fusion.61
  29.6 0.0 collective-permute-done.2
  29.6 0.3 fusion.57
  29.9 0.3 fusion.58
  30.1 0.8 %collective-permute-done.5 = bf16[192,768]{1,0:T(8,128)(2,1)S(1)} collective-permute-done((bf16[192,768]{1,0:T(8,128)(2,1)S(1)}, bf16[192,768]{1,0:T(8,128)(2,1)S(1)}, u32[]{:S(2)}, u32[]{:S(2)}) %collective-permute-start.5) | collective-permute-done | bytes 294944 | tf_op jit(solution)/shard_map/ppermute | solution.py:52
  30.9 0.3 fusion.59
  31.2 0.3 fusion.60
  31.5 0.1 add_select_fusion
  31.7 0.1 pad_maximum_fusion.4
  31.8 2.2 %collective-permute-start.9 = (f32[48,384]{1,0:T(8,128)S(1)}, f32[48,384]{1,0:T(8,128)S(1)}, u32[]{:S(2)}, u32[]{:S(2)}) collective-permute-start(f32[48,384]{1,0:T(8,128)S(1)} %pad_maximum_fusion.4), channel_id=1, source_target_pairs={{0,5},{4,12},{8,0},{12,4},{13,8},{9,1},{5,13},{1,9},{2,7},{6,14},{... | collective-permute-start | bytes 221192 | tf_op jit(solution)/shard_map/ppermute | solution.py:42
  34.1 0.1 pad_maximum_fusion.5
  34.1 0.7 %collective-permute-start.10 = (f32[48,384]{1,0:T(8,128)S(1)}, f32[48,384]{1,0:T(8,128)S(1)}, u32[]{:S(2)}, u32[]{:S(2)}) collective-permute-start(f32[48,384]{1,0:T(8,128)S(1)} %pad_maximum_fusion.5), channel_id=1, source_target_pairs={{0,7},{4,14},{8,2},{12,6},{13,10},{9,3},{5,15},{1,11},{2,5},{6,12}... | collective-permute-start | bytes 221192 | tf_op jit(solution)/shard_map/ppermute | solution.py:42
  34.8 0.1 pad_maximum_fusion.2
  34.9 0.5 %collective-permute-start.13 = (f32[96,384]{1,0:T(8,128)S(1)}, f32[96,384]{1,0:T(8,128)S(1)}, u32[]{:S(2)}, u32[]{:S(2)}) collective-permute-start(f32[96,384]{1,0:T(8,128)S(1)} %pad_maximum_fusion.2), channel_id=1, source_target_pairs={{0,1},{4,0},{8,4},{12,8},{13,12},{9,13},{5,9},{1,5},{2,3},{6,2},{1... | collective-permute-start | bytes 442376 | tf_op jit(solution)/shard_map/ppermute | solution.py:42
  35.4 0.1 pad_maximum_fusion.6
  35.5 3.0 %collective-permute-start.11 = (f32[48,384]{1,0:T(8,128)S(1)}, f32[48,384]{1,0:T(8,128)S(1)}, u32[]{:S(2)}, u32[]{:S(2)}) collective-permute-start(f32[48,384]{1,0:T(8,128)S(1)} %pad_maximum_fusion.6), channel_id=1, source_target_pairs={{0,6},{4,2},{8,10},{12,14},{13,11},{9,15},{5,7},{1,3},{2,4},{6,0},... | collective-permute-start | bytes 221192 | tf_op jit(solution)/shard_map/ppermute | solution.py:42
  38.5 0.0 collective-permute-done.9
  38.5 3.5 %collective-permute-done.10 = f32[48,384]{1,0:T(8,128)S(1)} collective-permute-done((f32[48,384]{1,0:T(8,128)S(1)}, f32[48,384]{1,0:T(8,128)S(1)}, u32[]{:S(2)}, u32[]{:S(2)}) %collective-permute-start.10) | collective-permute-done | bytes 73760 | tf_op jit(solution)/shard_map/ppermute | solution.py:42
  42.0 1.6 %collective-permute-done.11 = f32[48,384]{1,0:T(8,128)S(1)} collective-permute-done((f32[48,384]{1,0:T(8,128)S(1)}, f32[48,384]{1,0:T(8,128)S(1)}, u32[]{:S(2)}, u32[]{:S(2)}) %collective-permute-start.11) | collective-permute-done | bytes 73760 | tf_op jit(solution)/shard_map/ppermute | solution.py:42
  43.6 0.0 collective-permute-done.13
  43.6 0.1 fusion.56
  43.7 0.1 fusion.55
  43.8 0.1 slice_add_fusion
  43.9 0.1 fusion.5
  43.9 0.1 fusion.14
  44.1 0.1 collective-permute-start.14
  44.2 1.4 %collective-permute-done.14 = f32[4,48,192]{2,1,0:T(8,128)S(1)} collective-permute-done((f32[4,48,192]{2,1,0:T(8,128)S(1)}, f32[4,48,192]{2,1,0:T(8,128)S(1)}, u32[]{:S(2)}, u32[]{:S(2)}) %collective-permute-start.14) | collective-permute-done | bytes 147488 | tf_op jit(solution)/shard_map/ppermute | solution.py:52
  45.6 0.8 %maximum_multiply_fusion = f32[48,768]{1,0:T(8,128)} fusion(f32[48,192]{1,0:T(8,128)S(1)} %get-tuple-element.53, f32[48,192]{1,0:T(8,128)S(1)} %get-tuple-element.54, f32[48,192]{1,0:T(8,128)S(1)} %get-tuple-element.55, f32[48,192]{1,0:T(8,128)S(1)} %get-tuple-element.52), kind=kLoop, calls=%fused_computation.9 | loop fusion | flops 147456 | bytes 294912 | tf_op jit(solution)/shard_map/div | solution.py:118
  (23 shorter events, 0.6 us)
Async XLA Ops:
  0.0 6.7 %copy-start = (bf16[1,192,2048]{2,1,0:T(8,128)(2,1)S(1)}, bf16[1,192,2048]{2,1,0:T(8,128)(2,1)}, u32[]{:S(2)}) copy-start(bf16[1,192,2048]{2,1,0:T(8,128)(2,1)} %param.1) | copy-start | bytes 2359300
  1.1 15.5 %collective-permute-start = (bf16[192,768]{1,0:T(8,128)(2,1)S(1)}, bf16[192,768]{1,0:T(8,128)(2,1)S(1)}, u32[]{:S(2)}, u32[]{:S(2)}) collective-permute-start(bf16[192,768]{1,0:T(8,128)(2,1)S(1)} %slice.112), channel_id=1, source_target_pairs={{0,4},{4,8},{8,12},{12,13},{13,9},{9,5},{5,1},{1,0},{2,6},{6,10},{... | collective-permute-start | bytes 884744 | tf_op jit(solution)/shard_map/ppermute | solution.py:42
  5.1 12.0 %collective-permute-start.3 = (bf16[192,768]{1,0:T(8,128)(2,1)S(1)}, bf16[192,768]{1,0:T(8,128)(2,1)S(1)}, u32[]{:S(2)}, u32[]{:S(2)}) collective-permute-start(bf16[192,768]{1,0:T(8,128)(2,1)S(1)} %slice.113), channel_id=1, source_target_pairs={{0,4},{4,8},{8,12},{12,13},{13,9},{9,5},{5,1},{1,0},{2,6},{6,10},{... | collective-permute-start | bytes 884744 | tf_op jit(solution)/shard_map/ppermute | solution.py:42
  6.7 6.9 %collective-permute-start.6 = (bf16[192,512]{1,0:T(8,128)(2,1)S(1)}, bf16[192,512]{1,0:T(8,128)(2,1)S(1)}, u32[]{:S(2)}, u32[]{:S(2)}) collective-permute-start(bf16[192,512]{1,0:T(8,128)(2,1)S(1)} %slice.114), channel_id=1, source_target_pairs={{0,4},{4,8},{8,12},{12,13},{13,9},{9,5},{5,1},{1,0},{2,6},{6,10},{... | collective-permute-start | bytes 589832 | tf_op jit(solution)/shard_map/ppermute | solution.py:42
  13.9 8.8 %collective-permute-start.7 = (bf16[192,512]{1,0:T(8,128)(2,1)S(1)}, bf16[192,512]{1,0:T(8,128)(2,1)S(1)}, u32[]{:S(2)}, u32[]{:S(2)}) collective-permute-start(bf16[192,512]{1,0:T(8,128)(2,1)S(1)} %collective-permute-done.6), channel_id=1, source_target_pairs={{0,4},{4,8},{8,12},{12,13},{13,9},{9,5},{5,1},{1,0},{2,6},{6,10},{... | collective-permute-start | bytes 589832 | tf_op jit(solution)/shard_map/ppermute | solution.py:42
  17.9 7.0 %collective-permute-start.12 = (f32[3,96,192]{2,1,0:T(8,128)S(1)}, f32[3,96,192]{2,1,0:T(8,128)S(1)}, u32[]{:S(2)}, u32[]{:S(2)}) collective-permute-start(f32[3,96,192]{2,1,0:T(8,128)S(1)} %pad_maximum_fusion), channel_id=1, source_target_pairs={{0,2},{4,6},{8,10},{12,14},{13,15},{9,11},{5,7},{1,3},{2,0},{6,4},... | collective-permute-start | bytes 663560 | tf_op jit(solution)/shard_map/ppermute | solution.py:42
  19.5 5.8 %collective-permute-start.1 = (bf16[192,768]{1,0:T(8,128)(2,1)S(1)}, bf16[192,768]{1,0:T(8,128)(2,1)S(1)}, u32[]{:S(2)}, u32[]{:S(2)}) collective-permute-start(bf16[192,768]{1,0:T(8,128)(2,1)S(1)} %collective-permute-done), channel_id=1, source_target_pairs={{0,4},{4,8},{8,12},{12,13},{13,9},{9,5},{5,1},{1,0},{2,6},{6,10},{... | collective-permute-start | bytes 884744 | tf_op jit(solution)/shard_map/ppermute | solution.py:42
  21.1 7.4 %collective-permute-start.4 = (bf16[192,768]{1,0:T(8,128)(2,1)S(1)}, bf16[192,768]{1,0:T(8,128)(2,1)S(1)}, u32[]{:S(2)}, u32[]{:S(2)}) collective-permute-start(bf16[192,768]{1,0:T(8,128)(2,1)S(1)} %collective-permute-done.3), channel_id=1, source_target_pairs={{0,4},{4,8},{8,12},{12,13},{13,9},{9,5},{5,1},{1,0},{2,6},{6,10},{... | collective-permute-start | bytes 884744 | tf_op jit(solution)/shard_map/ppermute | solution.py:42
  22.9 6.1 %collective-permute-start.8 = (bf16[192,512]{1,0:T(8,128)(2,1)S(1)}, bf16[192,512]{1,0:T(8,128)(2,1)S(1)}, u32[]{:S(2)}, u32[]{:S(2)}) collective-permute-start(bf16[192,512]{1,0:T(8,128)(2,1)S(1)} %collective-permute-done.7), channel_id=1, source_target_pairs={{0,1},{1,0},{2,3},{3,2},{4,5},{5,4},{6,7},{7,6},{8,9},{9,8},{10,11... | collective-permute-start | bytes 589832 | tf_op jit(solution)/shard_map/ppermute | solution.py:52
  25.6 4.0 %collective-permute-start.2 = (bf16[192,768]{1,0:T(8,128)(2,1)S(1)}, bf16[192,768]{1,0:T(8,128)(2,1)S(1)}, u32[]{:S(2)}, u32[]{:S(2)}) collective-permute-start(bf16[192,768]{1,0:T(8,128)(2,1)S(1)} %collective-permute-done.1), channel_id=1, source_target_pairs={{0,1},{1,0},{2,3},{3,2},{4,5},{5,4},{6,7},{7,6},{8,9},{9,8},{10,11... | collective-permute-start | bytes 884744 | tf_op jit(solution)/shard_map/ppermute | solution.py:52
  29.3 1.6 %collective-permute-start.5 = (bf16[192,768]{1,0:T(8,128)(2,1)S(1)}, bf16[192,768]{1,0:T(8,128)(2,1)S(1)}, u32[]{:S(2)}, u32[]{:S(2)}) collective-permute-start(bf16[192,768]{1,0:T(8,128)(2,1)S(1)} %collective-permute-done.4), channel_id=1, source_target_pairs={{0,1},{1,0},{2,3},{3,2},{4,5},{5,4},{6,7},{7,6},{8,9},{9,8},{10,11... | collective-permute-start | bytes 884744 | tf_op jit(solution)/shard_map/ppermute | solution.py:52
  31.8 6.7 %collective-permute-start.9 = (f32[48,384]{1,0:T(8,128)S(1)}, f32[48,384]{1,0:T(8,128)S(1)}, u32[]{:S(2)}, u32[]{:S(2)}) collective-permute-start(f32[48,384]{1,0:T(8,128)S(1)} %pad_maximum_fusion.4), channel_id=1, source_target_pairs={{0,5},{4,12},{8,0},{12,4},{13,8},{9,1},{5,13},{1,9},{2,7},{6,14},{... | collective-permute-start | bytes 221192 | tf_op jit(solution)/shard_map/ppermute | solution.py:42
  34.1 7.9 %collective-permute-start.10 = (f32[48,384]{1,0:T(8,128)S(1)}, f32[48,384]{1,0:T(8,128)S(1)}, u32[]{:S(2)}, u32[]{:S(2)}) collective-permute-start(f32[48,384]{1,0:T(8,128)S(1)} %pad_maximum_fusion.5), channel_id=1, source_target_pairs={{0,7},{4,14},{8,2},{12,6},{13,10},{9,3},{5,15},{1,11},{2,5},{6,12}... | collective-permute-start | bytes 221192 | tf_op jit(solution)/shard_map/ppermute | solution.py:42
  34.9 8.6 %collective-permute-start.13 = (f32[96,384]{1,0:T(8,128)S(1)}, f32[96,384]{1,0:T(8,128)S(1)}, u32[]{:S(2)}, u32[]{:S(2)}) collective-permute-start(f32[96,384]{1,0:T(8,128)S(1)} %pad_maximum_fusion.2), channel_id=1, source_target_pairs={{0,1},{4,0},{8,4},{12,8},{13,12},{9,13},{5,9},{1,5},{2,3},{6,2},{1... | collective-permute-start | bytes 442376 | tf_op jit(solution)/shard_map/ppermute | solution.py:42
  35.5 8.1 %collective-permute-start.11 = (f32[48,384]{1,0:T(8,128)S(1)}, f32[48,384]{1,0:T(8,128)S(1)}, u32[]{:S(2)}, u32[]{:S(2)}) collective-permute-start(f32[48,384]{1,0:T(8,128)S(1)} %pad_maximum_fusion.6), channel_id=1, source_target_pairs={{0,6},{4,2},{8,10},{12,14},{13,11},{9,15},{5,7},{1,3},{2,4},{6,0},... | collective-permute-start | bytes 221192 | tf_op jit(solution)/shard_map/ppermute | solution.py:42
  44.1 1.5 %collective-permute-start.14 = (f32[4,48,192]{2,1,0:T(8,128)S(1)}, f32[4,48,192]{2,1,0:T(8,128)S(1)}, u32[]{:S(2)}, u32[]{:S(2)}) collective-permute-start(f32[4,48,192]{2,1,0:T(8,128)S(1)} %pad_maximum_fusion.1), channel_id=1, source_target_pairs={{0,1},{1,0},{2,3},{3,2},{4,5},{5,4},{6,7},{7,6},{8,9},{9,8},{10,11... | collective-permute-start | bytes 442376 | tf_op jit(solution)/shard_map/ppermute | solution.py:52

commit v4 on v3

--- a/solution.py
+++ b/solution.py
@@ -44,9 +44,6 @@
     def pack(value):
         return jnp.concatenate([value[:quarter], value[quarter:]], 1)
 
-    def unpack(value):
-        return jnp.concatenate([value[:, :width], value[:, width:]], 0)
-
     def swap(value):
         pairs = [(i, i ^ 1) for i in range(n * PG)]
         return lax.ppermute(value, "walker", pairs)
@@ -82,11 +79,11 @@
     early = jnp.stack(keep) + move(jnp.stack(send), turn(lambda r, q: r, 1))
     early = lax.optimization_barrier(early)
 
-    s3, s3t = products(own_parts, b_parts)
-    s4, s4t = products(p_parts, b_parts)
     lone = group_index == 1
-    far = jnp.where(lone, s4, s3t)
-    near = jnp.where(lone, s4t, s3)
+    held = [jnp.where(lone, there, here) for there, here in zip(p_parts, own_parts)]
+    forth, back = products(held, b_parts)
+    far = jnp.where(lone, forth, back)
+    near = jnp.where(lone, back, forth)
     far_keep, far_send = halves(far)
     near_keep, near_send = halves(near)
 
@@ -97,25 +94,37 @@
     y = move(pack(near_send), turn(lambda r, q: beside.get(r, r), 1))
     ez = move(jnp.concatenate([early[2], near_keep], 1), turn(lambda r, q: r - 1))
     x, xf, y, ez = lax.optimization_barrier((x, xf, y, ez))
-    x = unpack(x + xf)
-    y = unpack(y)
-    up1, z = ez[:, :width], ez[:, width:]
-    found = {0: early[0], -1: early[1], 1: up1, 2: x, -3: x, -2: near_keep + y, 3: z + y}
-    sign = 1 - 2 * core
+    x = x + xf
 
     def quarter_of(which):
+        def rows(v):
+            return lax.dynamic_slice_in_dim(v, which * quarter, quarter, 0)
+
+        def lanes(v):
+            return jnp.where(which == 0, v[:, :width], v[:, width:])
+
+        far_rows = lanes(x)
+        beside_rows = lanes(y)
+        found = {
+            0: rows(early[0]),
+            -1: rows(early[1]),
+            1: rows(ez[:, :width]),
+            2: far_rows,
+            -3: far_rows,
+            -2: rows(near_keep) + beside_rows,
+            3: rows(ez[:, width:]) + beside_rows,
+        }
         blocks = []
         for b in range(n):
             offset = sign * (b - pos)
-            value = None
+            value = found[0]
             for d, v in found.items():
-                v = lax.dynamic_slice_in_dim(v, which * quarter, quarter, 0)
-                value = v if value is None else jnp.where(offset == d, v, value)
+                value = jnp.where(offset == d, v, value) if d else value
             blocks.append(value)
-        return jnp.stack(blocks)
+        return jnp.concatenate(blocks, 1)
 
-    total = quarter_of(core) + swap(quarter_of(1 - core))
-    return jnp.concatenate([total[b] for b in range(n)], 1) / (cols * PG)
+    sign = 1 - 2 * core
+    return (quarter_of(core) + swap(quarter_of(1 - core))) / (cols * PG)
 
 
 def from_behind(block, axis, distance):
@@ -167,7 +176,7 @@
 
 
 SPAN = 4
-CUTS = (3, 6, 8)
+CUTS = (6, 14, 16)
 
 
 def solution(mesh):

time: 46.5 us -> 47.9 us (1.030)
  matrix products: 4.82 us -> 2.56 us
  waiting for transfers between devices: 16.7 us -> 18.9 us
  starting transfers between devices: 20.2 us -> 21.5 us
    dot_general x19 -> x10, matrix products: 4.82 us -> 2.56 us  [dot(): lax.dot_general(a, b, (((1,), (1,)), ((), ())), preferred_element_type=jn...]
    ppermute x11, waiting for transfers between devices: 14.5 us -> 16.3 us  [move(): return lax.ppermute(value, 'walker', pairs)]
    ppermute x11, starting transfers between devices: 19.9 us -> 21 us  [move(): return lax.ppermute(value, 'walker', pairs)]
  transfers between devices with their start and end apart: 15 -> 15, of which waited for: 8 -> 8; matrix products, arithmetic and copies ran while one was open for 13% -> 9% of each run, Pallas kernels for 0% -> 0%
where the time goes in v4:
time: 47.9 us; the launch traced here: 47.8 us
  starting transfers between devices  21.5 us (45%)
  waiting for transfers between devices  18.9 us (39%)
  local copies, waits for them, and re-layouts  2.65 us (6%)
  matrix products  2.56 us (5%)
  other arithmetic  1.81 us (4%)
    ppermute x11, starting transfers between devices, move(): return lax.ppermute(value, 'walker', pairs)  21 us
    ppermute x11, waiting for transfers between devices, move(): return lax.ppermute(value, 'walker', pairs)  16.3 us
    ppermute x4, waiting for transfers between devices, swap(): return lax.ppermute(value, 'walker', pairs)  2.62 us
    dot_general x10, matrix products, dot(): lax.dot_general(a, b, (((1,), (1,)), ((), ())), preferred_element_type=jn...  2.56 us
    slice x1, local copies, waits for them, and re-layouts, body(): own_parts = [own[:, spans[0][0]:spans[0][1]]]  1.05 us
    slice x2, local copies, waits for them, and re-layouts, body(): own_parts += [rest[:, lo:hi] for lo, hi in spans[1:]]  1.03 us
  transfers between devices with their start and end apart: 15, of which 8 were waited for; matrix products, arithmetic and copies ran while one was open for 9% of the time, Pallas kernels for 0%

profile of v4, /device:TPU:0, one launch (start us, length us, event | category | flops | bytes accessed | tf_op | source)
XLA Modules:
  0.0 47.8 jit_solution(4079376302906172844)
XLA Ops:
  0.0 0.0 copy-start
  0.0 1.1 %slice.104 = bf16[192,768]{1,0:T(8,128)(2,1)S(1)} slice(bf16[192,2048]{1,0:T(8,128)(2,1)} %bitcast.82), slice={[0:192], [0:768]} | slice | bytes 589824 | tf_op jit(solution)/shard_map/slice | solution.py:53
  1.1 3.1 %collective-permute-start = (bf16[192,768]{1,0:T(8,128)(2,1)S(1)}, bf16[192,768]{1,0:T(8,128)(2,1)S(1)}, u32[]{:S(2)}, u32[]{:S(2)}) collective-permute-start(bf16[192,768]{1,0:T(8,128)(2,1)S(1)} %slice.104), channel_id=1, source_target_pairs={{0,4},{4,8},{8,12},{12,13},{13,9},{9,5},{5,1},{1,0},{2,6},{6,10},{... | collective-permute-start | bytes 884744 | tf_op jit(solution)/shard_map/ppermute | solution.py:42
  4.1 1.0 %slice.105 = bf16[192,1024]{1,0:T(8,128)(2,1)S(1)} slice(bf16[192,2048]{1,0:T(8,128)(2,1)} %bitcast.83), slice={[0:192], [768:1792]} | slice | bytes 786432 | tf_op jit(solution)/shard_map/slice | solution.py:55
  5.2 1.6 %collective-permute-start.3 = (bf16[192,1024]{1,0:T(8,128)(2,1)S(1)}, bf16[192,1024]{1,0:T(8,128)(2,1)S(1)}, u32[]{:S(2)}, u32[]{:S(2)}) collective-permute-start(bf16[192,1024]{1,0:T(8,128)(2,1)S(1)} %slice.105), channel_id=1, source_target_pairs={{0,4},{4,8},{8,12},{12,13},{13,9},{9,5},{5,1},{1,0},{2,6},{6,10},{... | collective-permute-start | bytes 1179656 | tf_op jit(solution)/shard_map/ppermute | solution.py:42
  6.7 0.0 copy-done
  6.8 1.6 %collective-permute-start.6 = (bf16[192,256]{1,0:T(8,128)(2,1)S(1)}, bf16[192,256]{1,0:T(8,128)(2,1)S(1)}, u32[]{:S(2)}, u32[]{:S(2)}) collective-permute-start(bf16[192,256]{1,0:T(8,128)(2,1)S(1)} %slice.106), channel_id=1, source_target_pairs={{0,4},{4,8},{8,12},{12,13},{13,9},{9,5},{5,1},{1,0},{2,6},{6,10},{... | collective-permute-start | bytes 294920 | tf_op jit(solution)/shard_map/ppermute | solution.py:42
  8.4 0.4 fusion
  8.8 4.8 %collective-permute-done.6 = bf16[192,256]{1,0:T(8,128)(2,1)S(1)} collective-permute-done((bf16[192,256]{1,0:T(8,128)(2,1)S(1)}, bf16[192,256]{1,0:T(8,128)(2,1)S(1)}, u32[]{:S(2)}, u32[]{:S(2)}) %collective-permute-start.6) | collective-permute-done | bytes 98336 | tf_op jit(solution)/shard_map/ppermute | solution.py:42
  13.6 0.2 fusion.28
  13.8 2.5 %collective-permute-start.7 = (bf16[192,256]{1,0:T(8,128)(2,1)S(1)}, bf16[192,256]{1,0:T(8,128)(2,1)S(1)}, u32[]{:S(2)}, u32[]{:S(2)}) collective-permute-start(bf16[192,256]{1,0:T(8,128)(2,1)S(1)} %collective-permute-done.6), channel_id=1, source_target_pairs={{0,4},{4,8},{8,12},{12,13},{13,9},{9,5},{5,1},{1,0},{2,6},{6,10},{... | collective-permute-start | bytes 294920 | tf_op jit(solution)/shard_map/ppermute | solution.py:42
  16.3 0.2 fusion.30
  16.5 2.0 %collective-permute-done.7 = bf16[192,256]{1,0:T(8,128)(2,1)S(1)} collective-permute-done((bf16[192,256]{1,0:T(8,128)(2,1)S(1)}, bf16[192,256]{1,0:T(8,128)(2,1)S(1)}, u32[]{:S(2)}, u32[]{:S(2)}) %collective-permute-start.7) | collective-permute-done | bytes 98336 | tf_op jit(solution)/shard_map/ppermute | solution.py:42
  18.5 0.0 collective-permute-start.8
  18.5 0.0 collective-permute-done
  18.5 0.3 fusion.35
  18.8 0.3 fusion.33
  19.1 2.4 %collective-permute-start.1 = (bf16[192,768]{1,0:T(8,128)(2,1)S(1)}, bf16[192,768]{1,0:T(8,128)(2,1)S(1)}, u32[]{:S(2)}, u32[]{:S(2)}) collective-permute-start(bf16[192,768]{1,0:T(8,128)(2,1)S(1)} %collective-permute-done), channel_id=1, source_target_pairs={{0,4},{4,8},{8,12},{12,13},{13,9},{9,5},{5,1},{1,0},{2,6},{6,10},{... | collective-permute-start | bytes 884744 | tf_op jit(solution)/shard_map/ppermute | solution.py:42
  21.5 0.0 collective-permute-done.3
  21.5 0.3 fusion.40
  21.8 0.3 fusion.38
  22.3 1.6 %collective-permute-start.12 = (f32[3,96,192]{2,1,0:T(8,128)S(1)}, f32[3,96,192]{2,1,0:T(8,128)S(1)}, u32[]{:S(2)}, u32[]{:S(2)}) collective-permute-start(f32[3,96,192]{2,1,0:T(8,128)S(1)} %pad_maximum_fusion), channel_id=1, source_target_pairs={{0,2},{4,6},{8,10},{12,14},{13,15},{9,11},{5,7},{1,3},{2,0},{6,4},... | collective-permute-start | bytes 663560 | tf_op jit(solution)/shard_map/ppermute | solution.py:42
  23.9 1.6 %collective-permute-start.4 = (bf16[192,1024]{1,0:T(8,128)(2,1)S(1)}, bf16[192,1024]{1,0:T(8,128)(2,1)S(1)}, u32[]{:S(2)}, u32[]{:S(2)}) collective-permute-start(bf16[192,1024]{1,0:T(8,128)(2,1)S(1)} %collective-permute-done.3), channel_id=1, source_target_pairs={{0,4},{4,8},{8,12},{12,13},{13,9},{9,5},{5,1},{1,0},{2,6},{6,10},{... | collective-permute-start | bytes 1179656 | tf_op jit(solution)/shard_map/ppermute | solution.py:42
  25.5 0.0 collective-permute-done.8
  25.5 0.2 fusion.9
  25.6 0.1 copy.4
  25.8 0.0 collective-permute-done.1
  25.8 0.3 collective-permute-start.2
  26.1 3.3 %collective-permute-done.12 = f32[3,96,192]{2,1,0:T(8,128)S(1)} collective-permute-done((f32[3,96,192]{2,1,0:T(8,128)S(1)}, f32[3,96,192]{2,1,0:T(8,128)S(1)}, u32[]{:S(2)}, u32[]{:S(2)}) %collective-permute-start.12) | collective-permute-done | bytes 221216 | tf_op jit(solution)/shard_map/ppermute | solution.py:42
  29.4 1.3 %collective-permute-done.4 = bf16[192,1024]{1,0:T(8,128)(2,1)S(1)} collective-permute-done((bf16[192,1024]{1,0:T(8,128)(2,1)S(1)}, bf16[192,1024]{1,0:T(8,128)(2,1)S(1)}, u32[]{:S(2)}, u32[]{:S(2)}) %collective-permute-start.4) | collective-permute-done | bytes 393248 | tf_op jit(solution)/shard_map/ppermute | solution.py:42
  30.8 0.0 collective-permute-start.5
  30.8 0.0 collective-permute-done.2
  30.8 0.3 fusion.5
  31.1 0.1 copy.2
  31.2 1.3 %collective-permute-done.5 = bf16[192,1024]{1,0:T(8,128)(2,1)S(1)} collective-permute-done((bf16[192,1024]{1,0:T(8,128)(2,1)S(1)}, bf16[192,1024]{1,0:T(8,128)(2,1)S(1)}, u32[]{:S(2)}, u32[]{:S(2)}) %collective-permute-start.5) | collective-permute-done | bytes 393248 | tf_op jit(solution)/shard_map/ppermute | solution.py:49
  32.5 0.3 fusion.2
  32.8 0.1 copy.3
  33.0 0.1 broadcast_select_fusion
  33.1 0.1 pad_maximum_fusion.3
  33.2 2.2 %collective-permute-start.9 = (f32[48,384]{1,0:T(8,128)S(1)}, f32[48,384]{1,0:T(8,128)S(1)}, u32[]{:S(2)}, u32[]{:S(2)}) collective-permute-start(f32[48,384]{1,0:T(8,128)S(1)} %pad_maximum_fusion.3), channel_id=1, source_target_pairs={{0,5},{4,12},{8,0},{12,4},{13,8},{9,1},{5,13},{1,9},{2,7},{6,14},{... | collective-permute-start | bytes 221192 | tf_op jit(solution)/shard_map/ppermute | solution.py:42
  35.4 0.1 pad_maximum_fusion.4
  35.5 2.5 %collective-permute-start.10 = (f32[48,384]{1,0:T(8,128)S(1)}, f32[48,384]{1,0:T(8,128)S(1)}, u32[]{:S(2)}, u32[]{:S(2)}) collective-permute-start(f32[48,384]{1,0:T(8,128)S(1)} %pad_maximum_fusion.4), channel_id=1, source_target_pairs={{0,7},{4,14},{8,2},{12,6},{13,10},{9,3},{5,15},{1,11},{2,5},{6,12}... | collective-permute-start | bytes 221192 | tf_op jit(solution)/shard_map/ppermute | solution.py:42
  38.0 0.1 pad_maximum_fusion.1
  38.1 0.0 collective-permute-start.13
  38.1 0.1 pad_maximum_fusion.5
  38.2 2.0 %collective-permute-start.11 = (f32[48,384]{1,0:T(8,128)S(1)}, f32[48,384]{1,0:T(8,128)S(1)}, u32[]{:S(2)}, u32[]{:S(2)}) collective-permute-start(f32[48,384]{1,0:T(8,128)S(1)} %pad_maximum_fusion.5), channel_id=1, source_target_pairs={{0,6},{4,2},{8,10},{12,14},{13,11},{9,15},{5,7},{1,3},{2,4},{6,0},... | collective-permute-start | bytes 221192 | tf_op jit(solution)/shard_map/ppermute | solution.py:42
  40.1 0.0 collective-permute-done.9
  40.1 2.9 %collective-permute-done.10 = f32[48,384]{1,0:T(8,128)S(1)} collective-permute-done((f32[48,384]{1,0:T(8,128)S(1)}, f32[48,384]{1,0:T(8,128)S(1)}, u32[]{:S(2)}, u32[]{:S(2)}) %collective-permute-start.10) | collective-permute-done | bytes 73760 | tf_op jit(solution)/shard_map/ppermute | solution.py:42
  43.0 2.0 %collective-permute-done.11 = f32[48,384]{1,0:T(8,128)S(1)} collective-permute-done((f32[48,384]{1,0:T(8,128)S(1)}, f32[48,384]{1,0:T(8,128)S(1)}, u32[]{:S(2)}, u32[]{:S(2)}) %collective-permute-start.11) | collective-permute-done | bytes 73760 | tf_op jit(solution)/shard_map/ppermute | solution.py:42
  45.0 0.0 collective-permute-done.13
  45.0 0.1 fusion.43
  45.1 0.1 fusion.13
  45.3 0.1 fusion.21
  45.5 0.1 pad_maximum_fusion.2
  45.6 0.1 collective-permute-start.14
  45.7 1.3 %collective-permute-done.14 = f32[48,768]{1,0:T(8,128)S(1)} collective-permute-done((f32[48,768]{1,0:T(8,128)S(1)}, f32[48,768]{1,0:T(8,128)S(1)}, u32[]{:S(2)}, u32[]{:S(2)}) %collective-permute-start.14) | collective-permute-done | bytes 147488 | tf_op jit(solution)/shard_map/ppermute | solution.py:49
  47.0 0.8 %fusion.8 = f32[48,768]{1,0:T(8,128)} fusion(f32[48,768]{1,0:T(8,128)S(1)} %collective-permute-done.14, f32[48,192]{1,0:T(8,128)S(1)} %get-tuple-element.43, f32[48,192]{1,0:T(8,128)S(1)} %get-tuple-element.40, f32[48,192]{1,0:T(8,128)S(1)} %get-tuple-element.39, f32[48,192]{1,0:T(8,128)S(1)} %get-tuple-element.29), kind=kLoop, calls=%fused_computation.14 | loop fusion | flops 184320 | bytes 442368 | tf_op jit(solution)/shard_map/div | solution.py:127
  (18 shorter events, 0.5 us)
Async XLA Ops:
  0.0 6.7 %copy-start = (bf16[1,192,2048]{2,1,0:T(8,128)(2,1)S(1)}, bf16[1,192,2048]{2,1,0:T(8,128)(2,1)}, u32[]{:S(2)}) copy-start(bf16[1,192,2048]{2,1,0:T(8,128)(2,1)} %param.1) | copy-start | bytes 2359300
  1.1 17.5 %collective-permute-start = (bf16[192,768]{1,0:T(8,128)(2,1)S(1)}, bf16[192,768]{1,0:T(8,128)(2,1)S(1)}, u32[]{:S(2)}, u32[]{:S(2)}) collective-permute-start(bf16[192,768]{1,0:T(8,128)(2,1)S(1)} %slice.104), channel_id=1, source_target_pairs={{0,4},{4,8},{8,12},{12,13},{13,9},{9,5},{5,1},{1,0},{2,6},{6,10},{... | collective-permute-start | bytes 884744 | tf_op jit(solution)/shard_map/ppermute | solution.py:42
  5.2 16.3 %collective-permute-start.3 = (bf16[192,1024]{1,0:T(8,128)(2,1)S(1)}, bf16[192,1024]{1,0:T(8,128)(2,1)S(1)}, u32[]{:S(2)}, u32[]{:S(2)}) collective-permute-start(bf16[192,1024]{1,0:T(8,128)(2,1)S(1)} %slice.105), channel_id=1, source_target_pairs={{0,4},{4,8},{8,12},{12,13},{13,9},{9,5},{5,1},{1,0},{2,6},{6,10},{... | collective-permute-start | bytes 1179656 | tf_op jit(solution)/shard_map/ppermute | solution.py:42
  6.8 6.9 %collective-permute-start.6 = (bf16[192,256]{1,0:T(8,128)(2,1)S(1)}, bf16[192,256]{1,0:T(8,128)(2,1)S(1)}, u32[]{:S(2)}, u32[]{:S(2)}) collective-permute-start(bf16[192,256]{1,0:T(8,128)(2,1)S(1)} %slice.106), channel_id=1, source_target_pairs={{0,4},{4,8},{8,12},{12,13},{13,9},{9,5},{5,1},{1,0},{2,6},{6,10},{... | collective-permute-start | bytes 294920 | tf_op jit(solution)/shard_map/ppermute | solution.py:42
  13.8 4.7 %collective-permute-start.7 = (bf16[192,256]{1,0:T(8,128)(2,1)S(1)}, bf16[192,256]{1,0:T(8,128)(2,1)S(1)}, u32[]{:S(2)}, u32[]{:S(2)}) collective-permute-start(bf16[192,256]{1,0:T(8,128)(2,1)S(1)} %collective-permute-done.6), channel_id=1, source_target_pairs={{0,4},{4,8},{8,12},{12,13},{13,9},{9,5},{5,1},{1,0},{2,6},{6,10},{... | collective-permute-start | bytes 294920 | tf_op jit(solution)/shard_map/ppermute | solution.py:42
  18.5 6.9 %collective-permute-start.8 = (bf16[192,256]{1,0:T(8,128)(2,1)S(1)}, bf16[192,256]{1,0:T(8,128)(2,1)S(1)}, u32[]{:S(2)}, u32[]{:S(2)}) collective-permute-start(bf16[192,256]{1,0:T(8,128)(2,1)S(1)} %collective-permute-done.7), channel_id=1, source_target_pairs={{0,1},{1,0},{2,3},{3,2},{4,5},{5,4},{6,7},{7,6},{8,9},{9,8},{10,11... | collective-permute-start | bytes 294920 | tf_op jit(solution)/shard_map/ppermute | solution.py:49
  19.1 6.7 %collective-permute-start.1 = (bf16[192,768]{1,0:T(8,128)(2,1)S(1)}, bf16[192,768]{1,0:T(8,128)(2,1)S(1)}, u32[]{:S(2)}, u32[]{:S(2)}) collective-permute-start(bf16[192,768]{1,0:T(8,128)(2,1)S(1)} %collective-permute-done), channel_id=1, source_target_pairs={{0,4},{4,8},{8,12},{12,13},{13,9},{9,5},{5,1},{1,0},{2,6},{6,10},{... | collective-permute-start | bytes 884744 | tf_op jit(solution)/shard_map/ppermute | solution.py:42
  22.3 7.1 %collective-permute-start.12 = (f32[3,96,192]{2,1,0:T(8,128)S(1)}, f32[3,96,192]{2,1,0:T(8,128)S(1)}, u32[]{:S(2)}, u32[]{:S(2)}) collective-permute-start(f32[3,96,192]{2,1,0:T(8,128)S(1)} %pad_maximum_fusion), channel_id=1, source_target_pairs={{0,2},{4,6},{8,10},{12,14},{13,15},{9,11},{5,7},{1,3},{2,0},{6,4},... | collective-permute-start | bytes 663560 | tf_op jit(solution)/shard_map/ppermute | solution.py:42
  23.9 6.9 %collective-permute-start.4 = (bf16[192,1024]{1,0:T(8,128)(2,1)S(1)}, bf16[192,1024]{1,0:T(8,128)(2,1)S(1)}, u32[]{:S(2)}, u32[]{:S(2)}) collective-permute-start(bf16[192,1024]{1,0:T(8,128)(2,1)S(1)} %collective-permute-done.3), channel_id=1, source_target_pairs={{0,4},{4,8},{8,12},{12,13},{13,9},{9,5},{5,1},{1,0},{2,6},{6,10},{... | collective-permute-start | bytes 1179656 | tf_op jit(solution)/shard_map/ppermute | solution.py:42
  25.8 5.0 %collective-permute-start.2 = (bf16[192,768]{1,0:T(8,128)(2,1)S(1)}, bf16[192,768]{1,0:T(8,128)(2,1)S(1)}, u32[]{:S(2)}, u32[]{:S(2)}) collective-permute-start(bf16[192,768]{1,0:T(8,128)(2,1)S(1)} %collective-permute-done.1), channel_id=1, source_target_pairs={{0,1},{1,0},{2,3},{3,2},{4,5},{5,4},{6,7},{7,6},{8,9},{9,8},{10,11... | collective-permute-start | bytes 884744 | tf_op jit(solution)/shard_map/ppermute | solution.py:49
  30.8 1.7 %collective-permute-start.5 = (bf16[192,1024]{1,0:T(8,128)(2,1)S(1)}, bf16[192,1024]{1,0:T(8,128)(2,1)S(1)}, u32[]{:S(2)}, u32[]{:S(2)}) collective-permute-start(bf16[192,1024]{1,0:T(8,128)(2,1)S(1)} %collective-permute-done.4), channel_id=1, source_target_pairs={{0,1},{1,0},{2,3},{3,2},{4,5},{5,4},{6,7},{7,6},{8,9},{9,8},{10,11... | collective-permute-start | bytes 1179656 | tf_op jit(solution)/shard_map/ppermute | solution.py:49
  33.2 7.0 %collective-permute-start.9 = (f32[48,384]{1,0:T(8,128)S(1)}, f32[48,384]{1,0:T(8,128)S(1)}, u32[]{:S(2)}, u32[]{:S(2)}) collective-permute-start(f32[48,384]{1,0:T(8,128)S(1)} %pad_maximum_fusion.3), channel_id=1, source_target_pairs={{0,5},{4,12},{8,0},{12,4},{13,8},{9,1},{5,13},{1,9},{2,7},{6,14},{... | collective-permute-start | bytes 221192 | tf_op jit(solution)/shard_map/ppermute | solution.py:42
  35.5 7.6 %collective-permute-start.10 = (f32[48,384]{1,0:T(8,128)S(1)}, f32[48,384]{1,0:T(8,128)S(1)}, u32[]{:S(2)}, u32[]{:S(2)}) collective-permute-start(f32[48,384]{1,0:T(8,128)S(1)} %pad_maximum_fusion.4), channel_id=1, source_target_pairs={{0,7},{4,14},{8,2},{12,6},{13,10},{9,3},{5,15},{1,11},{2,5},{6,12}... | collective-permute-start | bytes 221192 | tf_op jit(solution)/shard_map/ppermute | solution.py:42
  38.1 7.0 %collective-permute-start.13 = (f32[96,384]{1,0:T(8,128)S(1)}, f32[96,384]{1,0:T(8,128)S(1)}, u32[]{:S(2)}, u32[]{:S(2)}) collective-permute-start(f32[96,384]{1,0:T(8,128)S(1)} %pad_maximum_fusion.1), channel_id=1, source_target_pairs={{0,1},{4,0},{8,4},{12,8},{13,12},{9,13},{5,9},{1,5},{2,3},{6,2},{1... | collective-permute-start | bytes 442376 | tf_op jit(solution)/shard_map/ppermute | solution.py:42
  38.2 6.9 %collective-permute-start.11 = (f32[48,384]{1,0:T(8,128)S(1)}, f32[48,384]{1,0:T(8,128)S(1)}, u32[]{:S(2)}, u32[]{:S(2)}) collective-permute-start(f32[48,384]{1,0:T(8,128)S(1)} %pad_maximum_fusion.5), channel_id=1, source_target_pairs={{0,6},{4,2},{8,10},{12,14},{13,11},{9,15},{5,7},{1,3},{2,4},{6,0},... | collective-permute-start | bytes 221192 | tf_op jit(solution)/shard_map/ppermute | solution.py:42
  45.6 1.4 %collective-permute-start.14 = (f32[48,768]{1,0:T(8,128)S(1)}, f32[48,768]{1,0:T(8,128)S(1)}, u32[]{:S(2)}, u32[]{:S(2)}) collective-permute-start(f32[48,768]{1,0:T(8,128)S(1)} %pad_maximum_fusion.2), channel_id=1, source_target_pairs={{0,1},{1,0},{2,3},{3,2},{4,5},{5,4},{6,7},{7,6},{8,9},{9,8},{10,11... | collective-permute-start | bytes 442376 | tf_op jit(solution)/shard_map/ppermute | solution.py:49
